TPU v7x, 512 devices: a whole 4x8x8 slice. The times are simulated.
512 devices in a mesh: grp: 2 (over y_lo), gx: 16 (over x, y_hi), gy: 16 (over z, core).
Axes of the slice: x: 4, y: 8 (y_hi: 4, y_lo: 2; y = y_hi * 2 + y_lo), z: 8, core: 2. Of those that a mesh axis runs over, the one named last changes fastest.
Arguments:
- velocity: float32 [3, 256, 256, 256], P(None, 'gy', 'gx', 'grp'), may hold values from -6 to 6
- stress: float32 [6, 256, 256, 256], P(None, 'gy', 'gx', 'grp'), may hold values from -6 to 6
- buoyancy: float32 [256, 256, 256], P('gy', 'gx', 'grp'), may hold values from 0.5 to 1.5
- lame_lambda: float32 [256, 256, 256], P('gy', 'gx', 'grp'), may hold values from 0.5 to 2
- shear_modulus: float32 [256, 256, 256], P('gy', 'gx', 'grp'), may hold values from 0.3 to 1.5
- pml_flag: int32 [16, 16, 2], P('gy', 'gx', 'grp'), may hold values 0 or 1
- profile_index: int32 [16, 16, 2], P('gy', 'gx', 'grp'), may hold values from 0 to 3
- damping_peak: float32 [4], replicated, may hold values from 0.3 to 1.5
Outputs:
- velocity_next: float32 [3, 256, 256, 256], P(None, 'gy', 'gx', 'grp')
- stress_next: float32 [6, 256, 256, 256], P(None, 'gy', 'gx', 'grp')
- strain_rate: bfloat16 [2, 6, 256, 256, 256], P(None, None, 'gy', 'gx', 'grp')
All inputs are finite; a program needn't handle non-finite values. No bound on the sum of `pml_flag` on one device may be relied on, other than what follows from the above.
Results may differ from a plain program's by a relative error of at most 0.002.
Values may be sent and summed in bfloat16 or wider, within the bound.
A program may use at most 64 MiB of HBM per device.

v0:
```python
import jax
import jax.numpy as jnp
from jax import lax
from jax.sharding import PartitionSpec as P

STEPS = 2


COEF_NEAR = 9.0 / 8.0
COEF_FAR = -1.0 / 24.0
TIME_STEP = 0.15


def extended(x, sides, width):
    for axis, dim in sides:
        count, length = (lax.axis_size(axis), x.shape[dim])
        up = [(i, (i + 1) % count) for i in range(count - 1)]
        down = [(j, i) for i, j in up]
        last = lax.slice_in_dim(x, length - width, length, axis=dim)
        first = lax.slice_in_dim(x, 0, width, axis=dim)
        before = lax.ppermute(last, axis, up)
        after = lax.ppermute(first, axis, down)
        x = jnp.concatenate([before, x, after], axis=dim)
    return x


def take_slice(padded, dimension, offset, length):
    return lax.slice_in_dim(padded, offset, offset + length, axis=dimension)


def difference(padded, dimension, forward):
    length = padded.shape[dimension] - 4
    if forward:
        return COEF_NEAR * (
            take_slice(padded, dimension, 3, length) - take_slice(padded, dimension, 2, length)
        ) + COEF_FAR * (
            take_slice(padded, dimension, 4, length) - take_slice(padded, dimension, 1, length)
        )
    return COEF_NEAR * (
        take_slice(padded, dimension, 2, length) - take_slice(padded, dimension, 1, length)
    ) + COEF_FAR * (
        take_slice(padded, dimension, 3, length) - take_slice(padded, dimension, 0, length)
    )


def join_group(grouped, local):
    return jnp.concatenate(
        [grouped[..., :2].astype(jnp.float32), local, grouped[..., -2:].astype(jnp.float32)], axis=3
    )


def motion_pads(velocity):
    grouped = extended(velocity.astype(jnp.bfloat16), (("grp", 3),), 2)
    across = join_group(grouped, velocity)
    joint = extended(velocity, (("gx", 2), ("gy", 1)), 2)
    depth_parts = (joint[0][:, 2:-2], joint[1][:, 2:-2], joint[2][:, 2:-2])
    rows_parts = (joint[0][2:-2], joint[1][2:-2], joint[2][2:-2])
    return (depth_parts, rows_parts, (across[0], across[1], across[2]))


def tensor_pads(stress):
    grouped = extended(stress[:3].astype(jnp.bfloat16), (("grp", 3),), 2)
    across = join_group(grouped, stress[:3])
    joint = extended(stress, (("gx", 2), ("gy", 1)), 2)
    depth_parts = (joint[2][:, 2:-2], joint[4][:, 2:-2], joint[5][:, 2:-2])
    rows_parts = (joint[1][2:-2], joint[3][2:-2], joint[4][2:-2])
    return (depth_parts, rows_parts, (across[0], across[1], across[2]))


def relax(old, increment, retain, divide):
    return (old * retain + TIME_STEP * increment) / divide


def on_device(
    velocity, stress, buoyancy, lame_lambda, shear_modulus, pml_flag, profile_index, damping_peak
):
    depth_cells = velocity.shape[1]
    table = jnp.arange(damping_peak.shape[0], dtype=jnp.int32)
    peak_value = jnp.sum(jnp.where(table == profile_index[0, 0, 0], damping_peak, 0.0))
    tile_rate = pml_flag[0, 0, 0].astype(jnp.float32) * peak_value
    start = lax.axis_index("gy") * depth_cells
    total_depth = depth_cells * lax.axis_size("gy")
    depth = (
        (start + jnp.arange(depth_cells, dtype=jnp.int32)).astype(jnp.float32) + 0.5
    ) / total_depth
    ramp = 0.5 + 0.5 * depth * depth
    damping = tile_rate * ramp[:, None, None]
    retain = 1.0 - 0.5 * TIME_STEP * damping
    divide = 1.0 + 0.5 * TIME_STEP * damping
    strain_steps = []
    for step_index in range(STEPS):
        tensor_depth, tensor_rows, tensor_across = tensor_pads(stress)
        force_x = (
            difference(tensor_across[0], 2, True)
            + difference(tensor_rows[0], 1, False)
            + difference(tensor_depth[0], 0, False)
        )
        force_y = (
            difference(tensor_across[1], 2, False)
            + difference(tensor_rows[1], 1, True)
            + difference(tensor_depth[1], 0, False)
        )
        force_z = (
            difference(tensor_across[2], 2, False)
            + difference(tensor_rows[2], 1, False)
            + difference(tensor_depth[2], 0, True)
        )
        velocity_x = relax(velocity[0], buoyancy * force_x, retain, divide)
        velocity_y = relax(velocity[1], buoyancy * force_y, retain, divide)
        velocity_z = relax(velocity[2], buoyancy * force_z, retain, divide)
        velocity = jnp.stack([velocity_x, velocity_y, velocity_z])
        motion_depth, motion_rows, motion_across = motion_pads(velocity)
        normal_x = difference(motion_across[0], 2, False)
        normal_y = difference(motion_rows[1], 1, False)
        normal_z = difference(motion_depth[2], 0, False)
        shear_xy = 0.5 * (
            difference(motion_rows[0], 1, True) + difference(motion_across[1], 2, True)
        )
        shear_xz = 0.5 * (
            difference(motion_depth[0], 0, True) + difference(motion_across[2], 2, True)
        )
        shear_yz = 0.5 * (
            difference(motion_depth[1], 0, True) + difference(motion_rows[2], 1, True)
        )
        dilation = normal_x + normal_y + normal_z
        stress = jnp.stack(
            [
                relax(
                    stress[0],
                    lame_lambda * dilation + 2.0 * shear_modulus * normal_x,
                    retain,
                    divide,
                ),
                relax(stress[1], 2.0 * shear_modulus * shear_xy, retain, divide),
                relax(stress[2], 2.0 * shear_modulus * shear_xz, retain, divide),
                relax(
                    stress[3],
                    lame_lambda * dilation + 2.0 * shear_modulus * normal_y,
                    retain,
                    divide,
                ),
                relax(stress[4], 2.0 * shear_modulus * shear_yz, retain, divide),
                relax(
                    stress[5],
                    lame_lambda * dilation + 2.0 * shear_modulus * normal_z,
                    retain,
                    divide,
                ),
            ]
        )
        strain_steps.append(
            jnp.stack([normal_x, shear_xy, shear_xz, normal_y, shear_yz, normal_z]).astype(
                jnp.bfloat16
            )
        )
    return (velocity, stress, jnp.stack(strain_steps))


def solution(mesh):
    return jax.shard_map(
        on_device,
        mesh=mesh,
        in_specs=(
            P(None, "gy", "gx", "grp"),
            P(None, "gy", "gx", "grp"),
            P("gy", "gx", "grp"),
            P("gy", "gx", "grp"),
            P("gy", "gx", "grp"),
            P("gy", "gx", "grp"),
            P("gy", "gx", "grp"),
            P(),
        ),
        out_specs=(
            P(None, "gy", "gx", "grp"),
            P(None, "gy", "gx", "grp"),
            P(None, None, "gy", "gx", "grp"),
        ),
        check_vma=False,
    )
```

profile of v0, /device:TPU:199, one launch (start us, length us, event | category | flops | bytes accessed | tf_op | source)
XLA Modules:
  0.0 123.5 jit_solution(4104019254542270243)
XLA Ops:
  0.6 1.2 fusion.194
  1.8 6.1 %collective-permute-start.3 = (f32[6,16,2,128]{3,2,1,0:T(2,128)S(1)}, f32[6,16,2,128]{3,2,1,0:T(2,128)S(1)}, u32[]{:S(2)}, u32[]{:S(2)}) collective-permute-start(f32[6,16,2,128]{3,2,1,0:T(2,128)S(1)} %get-tuple-element.69), channel_id=1, source_target_pairs={{16,0},{32,16},{48,32},{64,48},{80,64},{96,80},{112,96},{128,112},... | collective-permute-start | bytes 294920 | tf_op jit(solution)/shard_map/ppermute | solution.py:22
  8.0 1.9 %collective-permute-start.2 = (f32[6,16,2,128]{3,2,1,0:T(2,128)S(1)}, f32[6,16,2,128]{3,2,1,0:T(2,128)S(1)}, u32[]{:S(2)}, u32[]{:S(2)}) collective-permute-start(f32[6,16,2,128]{3,2,1,0:T(2,128)S(1)} %get-tuple-element.68), channel_id=1, source_target_pairs={{0,16},{16,32},{32,48},{48,64},{64,80},{80,96},{96,112},{112,128},... | collective-permute-start | bytes 294920 | tf_op jit(solution)/shard_map/ppermute | solution.py:21
  11.1 1.3 %collective-permute-start.1 = (bf16[3,16,16,2]{3,2,1,0:T(8,128)(2,1)S(1)}, bf16[3,16,16,2]{3,2,1,0:T(8,128)(2,1)S(1)}, u32[]{:S(2)}, u32[]{:S(2)}) collective-permute-start(bf16[3,16,16,2]{3,2,1,0:T(8,128)(2,1)S(1)} %get-tuple-element.97), channel_id=1, source_target_pairs={{256,0},{257,1},{258,2},{259,3},{260,4},{261,5},{262,6},{263,7},{2... | collective-permute-start | bytes 9224 | tf_op jit(solution)/shard_map/ppermute | solution.py:22
  12.4 4.0 %collective-permute-start = (bf16[3,16,16,2]{3,2,1,0:T(8,128)(2,1)S(1)}, bf16[3,16,16,2]{3,2,1,0:T(8,128)(2,1)S(1)}, u32[]{:S(2)}, u32[]{:S(2)}) collective-permute-start(bf16[3,16,16,2]{3,2,1,0:T(8,128)(2,1)S(1)} %get-tuple-element.96), channel_id=1, source_target_pairs={{0,256},{1,257},{2,258},{3,259},{4,260},{5,261},{6,262},{7,263},{8... | collective-permute-start | bytes 9224 | tf_op jit(solution)/shard_map/ppermute | solution.py:21
  22.2 3.4 %collective-permute-start.5 = (f32[6,2,20,128]{3,2,1,0:T(8,128)S(1)}, f32[6,2,20,128]{3,2,1,0:T(8,128)S(1)}, u32[]{:S(2)}, u32[]{:S(2)}) collective-permute-start(f32[6,2,20,128]{3,2,1,0:T(8,128)S(1)} %get-tuple-element.53), channel_id=1, source_target_pairs={{1,0},{2,1},{3,2},{4,3},{5,4},{6,5},{7,6},{8,7},{9,8},{10,9},{11,1... | collective-permute-start | bytes 368648 | tf_op jit(solution)/shard_map/ppermute | solution.py:22
  25.6 5.1 %collective-permute-start.4 = (f32[6,2,20,128]{3,2,1,0:T(8,128)S(1)}, f32[6,2,20,128]{3,2,1,0:T(8,128)S(1)}, u32[]{:S(2)}, u32[]{:S(2)}) collective-permute-start(f32[6,2,20,128]{3,2,1,0:T(8,128)S(1)} %get-tuple-element.52), channel_id=1, source_target_pairs={{0,1},{1,2},{2,3},{3,4},{4,5},{5,6},{6,7},{7,8},{8,9},{9,10},{10,1... | collective-permute-start | bytes 368648 | tf_op jit(solution)/shard_map/ppermute | solution.py:21
  31.6 1.2 collective-permute-done.4
  33.8 1.3 %collective-permute-start.7 = (bf16[3,16,16,2]{3,2,1,0:T(8,128)(2,1)S(1)}, bf16[3,16,16,2]{3,2,1,0:T(8,128)(2,1)S(1)}, u32[]{:S(2)}, u32[]{:S(2)}) collective-permute-start(bf16[3,16,16,2]{3,2,1,0:T(8,128)(2,1)S(1)} %get-tuple-element.95), channel_id=1, source_target_pairs={{256,0},{257,1},{258,2},{259,3},{260,4},{261,5},{262,6},{263,7},{2... | collective-permute-start | bytes 9224 | tf_op jit(solution)/shard_map/ppermute | solution.py:22
  35.1 4.0 %collective-permute-start.6 = (bf16[3,16,16,2]{3,2,1,0:T(8,128)(2,1)S(1)}, bf16[3,16,16,2]{3,2,1,0:T(8,128)(2,1)S(1)}, u32[]{:S(2)}, u32[]{:S(2)}) collective-permute-start(bf16[3,16,16,2]{3,2,1,0:T(8,128)(2,1)S(1)} %get-tuple-element.94), channel_id=1, source_target_pairs={{0,256},{1,257},{2,258},{3,259},{4,260},{5,261},{6,262},{7,263},{8... | collective-permute-start | bytes 9224 | tf_op jit(solution)/shard_map/ppermute | solution.py:21
  39.2 6.7 %collective-permute-start.9 = (f32[3,16,2,128]{3,2,1,0:T(2,128)S(1)}, f32[3,16,2,128]{3,2,1,0:T(2,128)S(1)}, u32[]{:S(2)}, u32[]{:S(2)}) collective-permute-start(f32[3,16,2,128]{3,2,1,0:T(2,128)S(1)} %get-tuple-element.89), channel_id=1, source_target_pairs={{16,0},{32,16},{48,32},{64,48},{80,64},{96,80},{112,96},{128,112},... | collective-permute-start | bytes 147464 | tf_op jit(solution)/shard_map/ppermute | solution.py:22
  45.9 1.9 %collective-permute-start.8 = (f32[3,16,2,128]{3,2,1,0:T(2,128)S(1)}, f32[3,16,2,128]{3,2,1,0:T(2,128)S(1)}, u32[]{:S(2)}, u32[]{:S(2)}) collective-permute-start(f32[3,16,2,128]{3,2,1,0:T(2,128)S(1)} %get-tuple-element.88), channel_id=1, source_target_pairs={{0,16},{16,32},{32,48},{48,64},{64,80},{80,96},{96,112},{112,128},... | collective-permute-start | bytes 147464 | tf_op jit(solution)/shard_map/ppermute | solution.py:21
  48.5 5.2 %collective-permute-done.8 = f32[3,16,2,128]{3,2,1,0:T(2,128)S(1)} collective-permute-done((f32[3,16,2,128]{3,2,1,0:T(2,128)S(1)}, f32[3,16,2,128]{3,2,1,0:T(2,128)S(1)}, u32[]{:S(2)}, u32[]{:S(2)}) %collective-permute-start.8) | collective-permute-done | bytes 49184 | tf_op jit(solution)/shard_map/ppermute | solution.py:21
  53.9 3.2 %collective-permute-start.11 = (f32[3,2,20,128]{3,2,1,0:T(8,128)S(1)}, f32[3,2,20,128]{3,2,1,0:T(8,128)S(1)}, u32[]{:S(2)}, u32[]{:S(2)}) collective-permute-start(f32[3,2,20,128]{3,2,1,0:T(8,128)S(1)} %get-tuple-element.85), channel_id=1, source_target_pairs={{1,0},{2,1},{3,2},{4,3},{5,4},{6,5},{7,6},{8,7},{9,8},{10,9},{11,1... | collective-permute-start | bytes 184328 | tf_op jit(solution)/shard_map/ppermute | solution.py:22
  57.1 6.3 %collective-permute-start.10 = (f32[3,2,20,128]{3,2,1,0:T(8,128)S(1)}, f32[3,2,20,128]{3,2,1,0:T(8,128)S(1)}, u32[]{:S(2)}, u32[]{:S(2)}) collective-permute-start(f32[3,2,20,128]{3,2,1,0:T(8,128)S(1)} %get-tuple-element.84), channel_id=1, source_target_pairs={{0,1},{1,2},{2,3},{3,4},{4,5},{5,6},{6,7},{7,8},{8,9},{9,10},{10,1... | collective-permute-start | bytes 184328 | tf_op jit(solution)/shard_map/ppermute | solution.py:21
  63.6 1.1 collective-permute-done.10
  67.2 1.3 %collective-permute-start.13 = (bf16[3,16,16,2]{3,2,1,0:T(8,128)(2,1)S(1)}, bf16[3,16,16,2]{3,2,1,0:T(8,128)(2,1)S(1)}, u32[]{:S(2)}, u32[]{:S(2)}) collective-permute-start(bf16[3,16,16,2]{3,2,1,0:T(8,128)(2,1)S(1)} %get-tuple-element.93), channel_id=1, source_target_pairs={{256,0},{257,1},{258,2},{259,3},{260,4},{261,5},{262,6},{263,7},{2... | collective-permute-start | bytes 9224 | tf_op jit(solution)/shard_map/ppermute | solution.py:22
  68.5 4.0 %collective-permute-start.12 = (bf16[3,16,16,2]{3,2,1,0:T(8,128)(2,1)S(1)}, bf16[3,16,16,2]{3,2,1,0:T(8,128)(2,1)S(1)}, u32[]{:S(2)}, u32[]{:S(2)}) collective-permute-start(bf16[3,16,16,2]{3,2,1,0:T(8,128)(2,1)S(1)} %get-tuple-element.92), channel_id=1, source_target_pairs={{0,256},{1,257},{2,258},{3,259},{4,260},{5,261},{6,262},{7,263},{8... | collective-permute-start | bytes 9224 | tf_op jit(solution)/shard_map/ppermute | solution.py:21
  72.6 1.9 %collective-permute-start.15 = (f32[6,16,2,128]{3,2,1,0:T(2,128)S(1)}, f32[6,16,2,128]{3,2,1,0:T(2,128)S(1)}, u32[]{:S(2)}, u32[]{:S(2)}) collective-permute-start(f32[6,16,2,128]{3,2,1,0:T(2,128)S(1)} %get-tuple-element.61), channel_id=1, source_target_pairs={{16,0},{32,16},{48,32},{64,48},{80,64},{96,80},{112,96},{128,112},... | collective-permute-start | bytes 294920 | tf_op jit(solution)/shard_map/ppermute | solution.py:22
  74.5 4.3 %collective-permute-start.14 = (f32[6,16,2,128]{3,2,1,0:T(2,128)S(1)}, f32[6,16,2,128]{3,2,1,0:T(2,128)S(1)}, u32[]{:S(2)}, u32[]{:S(2)}) collective-permute-start(f32[6,16,2,128]{3,2,1,0:T(2,128)S(1)} %get-tuple-element.60), channel_id=1, source_target_pairs={{0,16},{16,32},{32,48},{48,64},{64,80},{80,96},{96,112},{112,128},... | collective-permute-start | bytes 294920 | tf_op jit(solution)/shard_map/ppermute | solution.py:21
  80.0 3.0 %collective-permute-done.14 = f32[6,16,2,128]{3,2,1,0:T(2,128)S(1)} collective-permute-done((f32[6,16,2,128]{3,2,1,0:T(2,128)S(1)}, f32[6,16,2,128]{3,2,1,0:T(2,128)S(1)}, u32[]{:S(2)}, u32[]{:S(2)}) %collective-permute-start.14) | collective-permute-done | bytes 98336 | tf_op jit(solution)/shard_map/ppermute | solution.py:21
  83.0 1.9 %collective-permute-start.17 = (f32[6,2,20,128]{3,2,1,0:T(8,128)S(1)}, f32[6,2,20,128]{3,2,1,0:T(8,128)S(1)}, u32[]{:S(2)}, u32[]{:S(2)}) collective-permute-start(f32[6,2,20,128]{3,2,1,0:T(8,128)S(1)} %get-tuple-element.48), channel_id=1, source_target_pairs={{1,0},{2,1},{3,2},{4,3},{5,4},{6,5},{7,6},{8,7},{9,8},{10,9},{11,1... | collective-permute-start | bytes 368648 | tf_op jit(solution)/shard_map/ppermute | solution.py:22
  85.0 7.1 %collective-permute-start.16 = (f32[6,2,20,128]{3,2,1,0:T(8,128)S(1)}, f32[6,2,20,128]{3,2,1,0:T(8,128)S(1)}, u32[]{:S(2)}, u32[]{:S(2)}) collective-permute-start(f32[6,2,20,128]{3,2,1,0:T(8,128)S(1)} %get-tuple-element.47), channel_id=1, source_target_pairs={{0,1},{1,2},{2,3},{3,4},{4,5},{5,6},{6,7},{7,8},{8,9},{9,10},{10,1... | collective-permute-start | bytes 368648 | tf_op jit(solution)/shard_map/ppermute | solution.py:21
  92.9 1.2 collective-permute-done.16
  95.1 1.3 %collective-permute-start.19 = (bf16[3,16,16,2]{3,2,1,0:T(8,128)(2,1)S(1)}, bf16[3,16,16,2]{3,2,1,0:T(8,128)(2,1)S(1)}, u32[]{:S(2)}, u32[]{:S(2)}) collective-permute-start(bf16[3,16,16,2]{3,2,1,0:T(8,128)(2,1)S(1)} %get-tuple-element.91), channel_id=1, source_target_pairs={{256,0},{257,1},{258,2},{259,3},{260,4},{261,5},{262,6},{263,7},{2... | collective-permute-start | bytes 9224 | tf_op jit(solution)/shard_map/ppermute | solution.py:22
  96.4 4.0 %collective-permute-start.18 = (bf16[3,16,16,2]{3,2,1,0:T(8,128)(2,1)S(1)}, bf16[3,16,16,2]{3,2,1,0:T(8,128)(2,1)S(1)}, u32[]{:S(2)}, u32[]{:S(2)}) collective-permute-start(bf16[3,16,16,2]{3,2,1,0:T(8,128)(2,1)S(1)} %get-tuple-element.90), channel_id=1, source_target_pairs={{0,256},{1,257},{2,258},{3,259},{4,260},{5,261},{6,262},{7,263},{8... | collective-permute-start | bytes 9224 | tf_op jit(solution)/shard_map/ppermute | solution.py:21
  100.5 1.9 %collective-permute-start.21 = (f32[3,16,2,128]{3,2,1,0:T(2,128)S(1)}, f32[3,16,2,128]{3,2,1,0:T(2,128)S(1)}, u32[]{:S(2)}, u32[]{:S(2)}) collective-permute-start(f32[3,16,2,128]{3,2,1,0:T(2,128)S(1)} %get-tuple-element.87), channel_id=1, source_target_pairs={{16,0},{32,16},{48,32},{64,48},{80,64},{96,80},{112,96},{128,112},... | collective-permute-start | bytes 147464 | tf_op jit(solution)/shard_map/ppermute | solution.py:22
  102.4 4.3 %collective-permute-start.20 = (f32[3,16,2,128]{3,2,1,0:T(2,128)S(1)}, f32[3,16,2,128]{3,2,1,0:T(2,128)S(1)}, u32[]{:S(2)}, u32[]{:S(2)}) collective-permute-start(f32[3,16,2,128]{3,2,1,0:T(2,128)S(1)} %get-tuple-element.86), channel_id=1, source_target_pairs={{0,16},{16,32},{32,48},{48,64},{64,80},{80,96},{96,112},{112,128},... | collective-permute-start | bytes 147464 | tf_op jit(solution)/shard_map/ppermute | solution.py:21
  107.4 2.9 %collective-permute-done.20 = f32[3,16,2,128]{3,2,1,0:T(2,128)S(1)} collective-permute-done((f32[3,16,2,128]{3,2,1,0:T(2,128)S(1)}, f32[3,16,2,128]{3,2,1,0:T(2,128)S(1)}, u32[]{:S(2)}, u32[]{:S(2)}) %collective-permute-start.20) | collective-permute-done | bytes 49184 | tf_op jit(solution)/shard_map/ppermute | solution.py:21
  110.4 1.9 %collective-permute-start.23 = (f32[3,2,20,128]{3,2,1,0:T(8,128)S(1)}, f32[3,2,20,128]{3,2,1,0:T(8,128)S(1)}, u32[]{:S(2)}, u32[]{:S(2)}) collective-permute-start(f32[3,2,20,128]{3,2,1,0:T(8,128)S(1)} %get-tuple-element.83), channel_id=1, source_target_pairs={{1,0},{2,1},{3,2},{4,3},{5,4},{6,5},{7,6},{8,7},{9,8},{10,9},{11,1... | collective-permute-start | bytes 184328 | tf_op jit(solution)/shard_map/ppermute | solution.py:22
  112.4 7.3 %collective-permute-start.22 = (f32[3,2,20,128]{3,2,1,0:T(8,128)S(1)}, f32[3,2,20,128]{3,2,1,0:T(8,128)S(1)}, u32[]{:S(2)}, u32[]{:S(2)}) collective-permute-start(f32[3,2,20,128]{3,2,1,0:T(8,128)S(1)} %get-tuple-element.82), channel_id=1, source_target_pairs={{0,1},{1,2},{2,3},{3,4},{4,5},{5,6},{6,7},{7,8},{8,9},{9,10},{10,1... | collective-permute-start | bytes 184328 | tf_op jit(solution)/shard_map/ppermute | solution.py:21
  119.9 1.1 collective-permute-done.22
  (112 shorter events, 16.7 us)
Async XLA Ops:
  1.8 19.3 %collective-permute-start.3 = (f32[6,16,2,128]{3,2,1,0:T(2,128)S(1)}, f32[6,16,2,128]{3,2,1,0:T(2,128)S(1)}, u32[]{:S(2)}, u32[]{:S(2)}) collective-permute-start(f32[6,16,2,128]{3,2,1,0:T(2,128)S(1)} %get-tuple-element.69), channel_id=1, source_target_pairs={{16,0},{32,16},{48,32},{64,48},{80,64},{96,80},{112,96},{128,112},... | collective-permute-start | bytes 294920 | tf_op jit(solution)/shard_map/ppermute | solution.py:22
  8.0 13.1 %collective-permute-start.2 = (f32[6,16,2,128]{3,2,1,0:T(2,128)S(1)}, f32[6,16,2,128]{3,2,1,0:T(2,128)S(1)}, u32[]{:S(2)}, u32[]{:S(2)}) collective-permute-start(f32[6,16,2,128]{3,2,1,0:T(2,128)S(1)} %get-tuple-element.68), channel_id=1, source_target_pairs={{0,16},{16,32},{32,48},{48,64},{64,80},{80,96},{96,112},{112,128},... | collective-permute-start | bytes 294920 | tf_op jit(solution)/shard_map/ppermute | solution.py:21
  11.1 8.5 %collective-permute-start.1 = (bf16[3,16,16,2]{3,2,1,0:T(8,128)(2,1)S(1)}, bf16[3,16,16,2]{3,2,1,0:T(8,128)(2,1)S(1)}, u32[]{:S(2)}, u32[]{:S(2)}) collective-permute-start(bf16[3,16,16,2]{3,2,1,0:T(8,128)(2,1)S(1)} %get-tuple-element.97), channel_id=1, source_target_pairs={{256,0},{257,1},{258,2},{259,3},{260,4},{261,5},{262,6},{263,7},{2... | collective-permute-start | bytes 9224 | tf_op jit(solution)/shard_map/ppermute | solution.py:22
  12.4 7.3 %collective-permute-start = (bf16[3,16,16,2]{3,2,1,0:T(8,128)(2,1)S(1)}, bf16[3,16,16,2]{3,2,1,0:T(8,128)(2,1)S(1)}, u32[]{:S(2)}, u32[]{:S(2)}) collective-permute-start(bf16[3,16,16,2]{3,2,1,0:T(8,128)(2,1)S(1)} %get-tuple-element.96), channel_id=1, source_target_pairs={{0,256},{1,257},{2,258},{3,259},{4,260},{5,261},{6,262},{7,263},{8... | collective-permute-start | bytes 9224 | tf_op jit(solution)/shard_map/ppermute | solution.py:21
  19.7 1.0 slice-start
  21.0 1.1 copy-start
  22.2 9.4 %collective-permute-start.5 = (f32[6,2,20,128]{3,2,1,0:T(8,128)S(1)}, f32[6,2,20,128]{3,2,1,0:T(8,128)S(1)}, u32[]{:S(2)}, u32[]{:S(2)}) collective-permute-start(f32[6,2,20,128]{3,2,1,0:T(8,128)S(1)} %get-tuple-element.53), channel_id=1, source_target_pairs={{1,0},{2,1},{3,2},{4,3},{5,4},{6,5},{7,6},{8,7},{9,8},{10,9},{11,1... | collective-permute-start | bytes 368648 | tf_op jit(solution)/shard_map/ppermute | solution.py:22
  25.6 7.2 %collective-permute-start.4 = (f32[6,2,20,128]{3,2,1,0:T(8,128)S(1)}, f32[6,2,20,128]{3,2,1,0:T(8,128)S(1)}, u32[]{:S(2)}, u32[]{:S(2)}) collective-permute-start(f32[6,2,20,128]{3,2,1,0:T(8,128)S(1)} %get-tuple-element.52), channel_id=1, source_target_pairs={{0,1},{1,2},{2,3},{3,4},{4,5},{5,6},{6,7},{7,8},{8,9},{9,10},{10,1... | collective-permute-start | bytes 368648 | tf_op jit(solution)/shard_map/ppermute | solution.py:21
  30.9 2.1 %copy-start.2 = (f32[16,16,128]{2,1,0:T(8,128)S(1)}, f32[16,16,128]{2,1,0:T(8,128)}, u32[]{:S(2)}) copy-start(f32[16,16,128]{2,1,0:T(8,128)} %param.10) | copy-start | bytes 393220
  30.9 2.1 %copy-start.5 = (f32[3,16,16,128]{3,2,1,0:T(8,128)S(1)}, f32[3,16,16,128]{3,2,1,0:T(8,128)}, u32[]{:S(2)}) copy-start(f32[3,16,16,128]{3,2,1,0:T(8,128)} %param.8) | copy-start | bytes 1179652
  33.8 13.9 %collective-permute-start.7 = (bf16[3,16,16,2]{3,2,1,0:T(8,128)(2,1)S(1)}, bf16[3,16,16,2]{3,2,1,0:T(8,128)(2,1)S(1)}, u32[]{:S(2)}, u32[]{:S(2)}) collective-permute-start(bf16[3,16,16,2]{3,2,1,0:T(8,128)(2,1)S(1)} %get-tuple-element.95), channel_id=1, source_target_pairs={{256,0},{257,1},{258,2},{259,3},{260,4},{261,5},{262,6},{263,7},{2... | collective-permute-start | bytes 9224 | tf_op jit(solution)/shard_map/ppermute | solution.py:22
  35.1 12.7 %collective-permute-start.6 = (bf16[3,16,16,2]{3,2,1,0:T(8,128)(2,1)S(1)}, bf16[3,16,16,2]{3,2,1,0:T(8,128)(2,1)S(1)}, u32[]{:S(2)}, u32[]{:S(2)}) collective-permute-start(bf16[3,16,16,2]{3,2,1,0:T(8,128)(2,1)S(1)} %get-tuple-element.94), channel_id=1, source_target_pairs={{0,256},{1,257},{2,258},{3,259},{4,260},{5,261},{6,262},{7,263},{8... | collective-permute-start | bytes 9224 | tf_op jit(solution)/shard_map/ppermute | solution.py:21
  39.2 9.3 %collective-permute-start.9 = (f32[3,16,2,128]{3,2,1,0:T(2,128)S(1)}, f32[3,16,2,128]{3,2,1,0:T(2,128)S(1)}, u32[]{:S(2)}, u32[]{:S(2)}) collective-permute-start(f32[3,16,2,128]{3,2,1,0:T(2,128)S(1)} %get-tuple-element.89), channel_id=1, source_target_pairs={{16,0},{32,16},{48,32},{64,48},{80,64},{96,80},{112,96},{128,112},... | collective-permute-start | bytes 147464 | tf_op jit(solution)/shard_map/ppermute | solution.py:22
  45.9 7.8 %collective-permute-start.8 = (f32[3,16,2,128]{3,2,1,0:T(2,128)S(1)}, f32[3,16,2,128]{3,2,1,0:T(2,128)S(1)}, u32[]{:S(2)}, u32[]{:S(2)}) collective-permute-start(f32[3,16,2,128]{3,2,1,0:T(2,128)S(1)} %get-tuple-element.88), channel_id=1, source_target_pairs={{0,16},{16,32},{32,48},{48,64},{64,80},{80,96},{96,112},{112,128},... | collective-permute-start | bytes 147464 | tf_op jit(solution)/shard_map/ppermute | solution.py:21
  53.9 9.8 %collective-permute-start.11 = (f32[3,2,20,128]{3,2,1,0:T(8,128)S(1)}, f32[3,2,20,128]{3,2,1,0:T(8,128)S(1)}, u32[]{:S(2)}, u32[]{:S(2)}) collective-permute-start(f32[3,2,20,128]{3,2,1,0:T(8,128)S(1)} %get-tuple-element.85), channel_id=1, source_target_pairs={{1,0},{2,1},{3,2},{4,3},{5,4},{6,5},{7,6},{8,7},{9,8},{10,9},{11,1... | collective-permute-start | bytes 184328 | tf_op jit(solution)/shard_map/ppermute | solution.py:22
  57.1 7.7 %collective-permute-start.10 = (f32[3,2,20,128]{3,2,1,0:T(8,128)S(1)}, f32[3,2,20,128]{3,2,1,0:T(8,128)S(1)}, u32[]{:S(2)}, u32[]{:S(2)}) collective-permute-start(f32[3,2,20,128]{3,2,1,0:T(8,128)S(1)} %get-tuple-element.84), channel_id=1, source_target_pairs={{0,1},{1,2},{2,3},{3,4},{4,5},{5,6},{6,7},{7,8},{8,9},{9,10},{10,1... | collective-permute-start | bytes 184328 | tf_op jit(solution)/shard_map/ppermute | solution.py:21
  65.4 0.9 copy-start.1
  65.4 1.0 copy-start.4
  67.2 11.6 %collective-permute-start.13 = (bf16[3,16,16,2]{3,2,1,0:T(8,128)(2,1)S(1)}, bf16[3,16,16,2]{3,2,1,0:T(8,128)(2,1)S(1)}, u32[]{:S(2)}, u32[]{:S(2)}) collective-permute-start(bf16[3,16,16,2]{3,2,1,0:T(8,128)(2,1)S(1)} %get-tuple-element.93), channel_id=1, source_target_pairs={{256,0},{257,1},{258,2},{259,3},{260,4},{261,5},{262,6},{263,7},{2... | collective-permute-start | bytes 9224 | tf_op jit(solution)/shard_map/ppermute | solution.py:22
  68.5 10.3 %collective-permute-start.12 = (bf16[3,16,16,2]{3,2,1,0:T(8,128)(2,1)S(1)}, bf16[3,16,16,2]{3,2,1,0:T(8,128)(2,1)S(1)}, u32[]{:S(2)}, u32[]{:S(2)}) collective-permute-start(bf16[3,16,16,2]{3,2,1,0:T(8,128)(2,1)S(1)} %get-tuple-element.92), channel_id=1, source_target_pairs={{0,256},{1,257},{2,258},{3,259},{4,260},{5,261},{6,262},{7,263},{8... | collective-permute-start | bytes 9224 | tf_op jit(solution)/shard_map/ppermute | solution.py:21
  72.6 7.4 %collective-permute-start.15 = (f32[6,16,2,128]{3,2,1,0:T(2,128)S(1)}, f32[6,16,2,128]{3,2,1,0:T(2,128)S(1)}, u32[]{:S(2)}, u32[]{:S(2)}) collective-permute-start(f32[6,16,2,128]{3,2,1,0:T(2,128)S(1)} %get-tuple-element.61), channel_id=1, source_target_pairs={{16,0},{32,16},{48,32},{64,48},{80,64},{96,80},{112,96},{128,112},... | collective-permute-start | bytes 294920 | tf_op jit(solution)/shard_map/ppermute | solution.py:22
  74.5 8.5 %collective-permute-start.14 = (f32[6,16,2,128]{3,2,1,0:T(2,128)S(1)}, f32[6,16,2,128]{3,2,1,0:T(2,128)S(1)}, u32[]{:S(2)}, u32[]{:S(2)}) collective-permute-start(f32[6,16,2,128]{3,2,1,0:T(2,128)S(1)} %get-tuple-element.60), channel_id=1, source_target_pairs={{0,16},{16,32},{32,48},{48,64},{64,80},{80,96},{96,112},{112,128},... | collective-permute-start | bytes 294920 | tf_op jit(solution)/shard_map/ppermute | solution.py:21
  83.0 9.9 %collective-permute-start.17 = (f32[6,2,20,128]{3,2,1,0:T(8,128)S(1)}, f32[6,2,20,128]{3,2,1,0:T(8,128)S(1)}, u32[]{:S(2)}, u32[]{:S(2)}) collective-permute-start(f32[6,2,20,128]{3,2,1,0:T(8,128)S(1)} %get-tuple-element.48), channel_id=1, source_target_pairs={{1,0},{2,1},{3,2},{4,3},{5,4},{6,5},{7,6},{8,7},{9,8},{10,9},{11,1... | collective-permute-start | bytes 368648 | tf_op jit(solution)/shard_map/ppermute | solution.py:22
  85.0 9.1 %collective-permute-start.16 = (f32[6,2,20,128]{3,2,1,0:T(8,128)S(1)}, f32[6,2,20,128]{3,2,1,0:T(8,128)S(1)}, u32[]{:S(2)}, u32[]{:S(2)}) collective-permute-start(f32[6,2,20,128]{3,2,1,0:T(8,128)S(1)} %get-tuple-element.47), channel_id=1, source_target_pairs={{0,1},{1,2},{2,3},{3,4},{4,5},{5,6},{6,7},{7,8},{8,9},{9,10},{10,1... | collective-permute-start | bytes 368648 | tf_op jit(solution)/shard_map/ppermute | solution.py:21
  95.0 5.5 %copy-start.3 = (f32[3,16,16,128]{3,2,1,0:T(8,128)}, f32[3,16,16,128]{3,2,1,0:T(8,128)S(1)}, u32[]{:S(2)}) copy-start(f32[3,16,16,128]{3,2,1,0:T(8,128)S(1)} %get-tuple-element.30) | copy-start | bytes 1179652
  95.1 11.6 %collective-permute-start.19 = (bf16[3,16,16,2]{3,2,1,0:T(8,128)(2,1)S(1)}, bf16[3,16,16,2]{3,2,1,0:T(8,128)(2,1)S(1)}, u32[]{:S(2)}, u32[]{:S(2)}) collective-permute-start(bf16[3,16,16,2]{3,2,1,0:T(8,128)(2,1)S(1)} %get-tuple-element.91), channel_id=1, source_target_pairs={{256,0},{257,1},{258,2},{259,3},{260,4},{261,5},{262,6},{263,7},{2... | collective-permute-start | bytes 9224 | tf_op jit(solution)/shard_map/ppermute | solution.py:22
  96.4 10.3 %collective-permute-start.18 = (bf16[3,16,16,2]{3,2,1,0:T(8,128)(2,1)S(1)}, bf16[3,16,16,2]{3,2,1,0:T(8,128)(2,1)S(1)}, u32[]{:S(2)}, u32[]{:S(2)}) collective-permute-start(bf16[3,16,16,2]{3,2,1,0:T(8,128)(2,1)S(1)} %get-tuple-element.90), channel_id=1, source_target_pairs={{0,256},{1,257},{2,258},{3,259},{4,260},{5,261},{6,262},{7,263},{8... | collective-permute-start | bytes 9224 | tf_op jit(solution)/shard_map/ppermute | solution.py:21
  100.5 6.9 %collective-permute-start.21 = (f32[3,16,2,128]{3,2,1,0:T(2,128)S(1)}, f32[3,16,2,128]{3,2,1,0:T(2,128)S(1)}, u32[]{:S(2)}, u32[]{:S(2)}) collective-permute-start(f32[3,16,2,128]{3,2,1,0:T(2,128)S(1)} %get-tuple-element.87), channel_id=1, source_target_pairs={{16,0},{32,16},{48,32},{64,48},{80,64},{96,80},{112,96},{128,112},... | collective-permute-start | bytes 147464 | tf_op jit(solution)/shard_map/ppermute | solution.py:22
  102.4 7.8 %collective-permute-start.20 = (f32[3,16,2,128]{3,2,1,0:T(2,128)S(1)}, f32[3,16,2,128]{3,2,1,0:T(2,128)S(1)}, u32[]{:S(2)}, u32[]{:S(2)}) collective-permute-start(f32[3,16,2,128]{3,2,1,0:T(2,128)S(1)} %get-tuple-element.86), channel_id=1, source_target_pairs={{0,16},{16,32},{32,48},{48,64},{64,80},{80,96},{96,112},{112,128},... | collective-permute-start | bytes 147464 | tf_op jit(solution)/shard_map/ppermute | solution.py:21
  110.4 9.5 %collective-permute-start.23 = (f32[3,2,20,128]{3,2,1,0:T(8,128)S(1)}, f32[3,2,20,128]{3,2,1,0:T(8,128)S(1)}, u32[]{:S(2)}, u32[]{:S(2)}) collective-permute-start(f32[3,2,20,128]{3,2,1,0:T(8,128)S(1)} %get-tuple-element.83), channel_id=1, source_target_pairs={{1,0},{2,1},{3,2},{4,3},{5,4},{6,5},{7,6},{8,7},{9,8},{10,9},{11,1... | collective-permute-start | bytes 184328 | tf_op jit(solution)/shard_map/ppermute | solution.py:22
  112.4 8.7 %collective-permute-start.22 = (f32[3,2,20,128]{3,2,1,0:T(8,128)S(1)}, f32[3,2,20,128]{3,2,1,0:T(8,128)S(1)}, u32[]{:S(2)}, u32[]{:S(2)}) collective-permute-start(f32[3,2,20,128]{3,2,1,0:T(8,128)S(1)} %get-tuple-element.82), channel_id=1, source_target_pairs={{0,1},{1,2},{2,3},{3,4},{4,5},{5,6},{6,7},{7,8},{8,9},{9,10},{10,1... | collective-permute-start | bytes 184328 | tf_op jit(solution)/shard_map/ppermute | solution.py:21
  122.4 1.1 copy-start.6
  (1 other events, 0.7 us)
where the time goes:
time: 124 us
  starting transfers between devices  86.4 us (70%)
  waiting for transfers between devices  18 us (15%)
  other arithmetic  8.74 us (7%)
  local copies, waits for them, and re-layouts  6.92 us (6%)
  between operations  3.42 us (3%)
    ppermute x12, starting transfers between devices, extended(): before = lax.ppermute(last, axis, up)  54.1 us
    ppermute x12, starting transfers between devices, extended(): after = lax.ppermute(first, axis, down)  32.3 us
    ppermute x12, waiting for transfers between devices, extended(): before = lax.ppermute(last, axis, up)  15.8 us
    unnamed x20, other arithmetic  2.74 us
    unnamed x16, local copies, waits for them, and re-layouts  2.74 us
  transfers between devices with their start and end apart: 24, of which 10 were waited for; matrix products, arithmetic and copies ran while one was open for 4% of the time, Pallas kernels for 0%

commit v1 on v0

v1 whole, which is shorter than its diff:
```python
import functools

import jax
import jax.numpy as jnp
from jax import lax
from jax.experimental import pallas as pl
from jax.experimental.pallas import tpu as pltpu
from jax.sharding import PartitionSpec as P

MESH = pl.DeviceIdType.MESH
F32 = jnp.float32
BF16 = jnp.bfloat16

STEPS = 2
NEAR = 9.0 / 8.0
RATIO = -1.0 / 27.0
TIME_STEP = 0.15
HALF = 0.5 * TIME_STEP

EDGE = 2

STRESS = {
    "x": ((0, True), (1, False), (2, False)),
    "y": ((1, False), (3, True), (4, False)),
    "z": ((2, False), (4, False), (5, True)),
}
MOTION = {
    "x": ((0, False), (1, True), (2, True)),
    "y": ((0, True), (1, False), (2, True)),
    "z": ((0, True), (1, True), (2, False)),
}


def row_list(kind, upward):
    rows = []
    for slot, (field, forward) in enumerate(kind["y"]):
        rows.append((slot, field, 0))
    for slot, (field, forward) in enumerate(kind["y"]):
        if forward != upward:
            rows.append((slot, field, 1))
    return rows


def kernel(
    depth, rows, lanes,
    vel_hbm, str_hbm, buoy_hbm, lam_hbm, mu_hbm, flag_ref, prof_ref, peak_ref,
    vout_hbm, sout_hbm, eout_hbm,
    s0, s1, v1, v2, sfin, vin, buoy, lam, mu, keep_ref, gain_ref, cross, strain, eout,
    up_send, up_recv, dn_send, dn_recv, grp_send, grp_recv,
    in_sem, out_sem, ysend_sem, yrecv_sem, zsend_sem, zrecv_sem, gsend_sem, grecv_sem,
):
    gx, gy, grp = lax.axis_index("gx"), lax.axis_index("gy"), lax.axis_index("grp")
    n_gx, n_gy = lax.axis_size("gx"), lax.axis_size("gy")
    has_prev_y, has_next_y = gx > 0, gx < n_gx - 1
    has_prev_z, has_next_z = gy > 0, gy < n_gy - 1
    prev_y, next_y = {"gx": gx - 1}, {"gx": gx + 1}
    prev_z, next_z = {"gy": gy - 1}, {"gy": gy + 1}
    other = {"grp": 1 - grp}

    barrier = pltpu.get_barrier_semaphore()

    def greet(device):
        pl.semaphore_signal(barrier, inc=1, device_id=device, device_id_type=MESH)

    greet(other)
    for exists, device in (
        (has_prev_y, prev_y), (has_next_y, next_y), (has_prev_z, prev_z), (has_next_z, next_z),
    ):
        pl.when(exists)(functools.partial(greet, device))

    def planes(ref, field, first, count):
        return ref.at[field, pl.ds(first * rows, count * rows), :]

    def interior(ref, field):
        return planes(ref, field, EDGE, depth)

    def plane(p):
        return pl.ds(pl.multiple_of(p * rows, 8), rows)

    loads = []

    def load(src, dst):
        copy = pltpu.make_async_copy(src, dst, in_sem.at[len(loads)])
        copy.start()
        loads.append(copy)
        return copy

    stress_load = {f: load(str_hbm.at[f], interior(s0, f)) for f in (1, 3, 4, 0, 2, 5)}
    buoy_load = load(buoy_hbm, buoy)
    vel_load = load(vel_hbm, vin)
    lam_load = load(lam_hbm, lam)
    mu_load = load(mu_hbm, mu)

    z_fields = ((s0, (2, 4, 5)), (s1, (2, 4, 5)), (v1, (0, 1, 2)), (v2, (0, 1, 2)))

    def clear_planes(first):
        for ref, fields in z_fields:
            for f in fields:
                ref[f, pl.ds(first * rows, EDGE * rows), :] = jnp.zeros((EDGE * rows, lanes), F32)

    pl.when(jnp.logical_not(has_prev_z))(functools.partial(clear_planes, 0))
    pl.when(jnp.logical_not(has_next_z))(functools.partial(clear_planes, EDGE + depth))

    def clear_recv(ref):
        ref[...] = jnp.zeros_like(ref)

    pl.when(jnp.logical_not(has_prev_y))(functools.partial(clear_recv, up_recv))
    pl.when(jnp.logical_not(has_next_y))(functools.partial(clear_recv, dn_recv))

    choice = prof_ref[0, 0, 0]
    peak = jnp.float32(0.0)
    for i in range(peak_ref.shape[0]):
        peak = peak + jnp.where(choice == i, peak_ref[i], 0.0)
    rate = flag_ref[0, 0, 0].astype(F32) * peak

    def damping_of(shape):
        z = (lax.broadcasted_iota(jnp.int32, shape, 0) + gy * depth).astype(F32)
        q = (z + 0.5) / (depth * n_gy)
        damping = rate * (0.5 + 0.5 * q * q)
        divide = 1.0 + HALF * damping
        return (1.0 - HALF * damping) / divide, (NEAR * TIME_STEP) / divide

    keep_ref[...], gain_ref[...] = damping_of((depth, 8, lanes))

    slot = lax.broadcasted_iota(jnp.int32, (8, lanes), 0)
    lane = lax.broadcasted_iota(jnp.int32, (8, lanes), 1)
    near_lane = jnp.where(grp == 0, lanes - 1, 0)
    far_lane = jnp.where(grp == 0, lanes - 2, 1)

    def picker(k):
        hit = ((slot == 2 * k) & (lane == near_lane)) | ((slot == 2 * k + 1) & (lane == far_lane))
        return jnp.where(hit, 1.0, 0.0).astype(BF16)

    def placer(k, forward):
        near, far = slot == 2 * k, slot == 2 * k + 1
        if forward:
            one = (near & (lane == lanes - 1)) & (grp == 0)
            after = ((near & (lane == lanes - 2)) | (far & (lane == lanes - 1))) & (grp == 0)
            before = (near & (lane == 0)) & (grp == 1)
            whole = jnp.where(one, 1.0, 0.0)
        else:
            one = (near & (lane == 0)) & (grp == 1)
            after = (near & (lane == lanes - 1)) & (grp == 0)
            before = ((near & (lane == 1)) | (far & (lane == 0))) & (grp == 1)
            whole = jnp.where(one, -1.0, 0.0)
        part = jnp.where(after, RATIO, jnp.where(before, -RATIO, 0.0))
        high = part.astype(BF16)
        low = (part - high.astype(F32)).astype(BF16)
        return jnp.concatenate([whole.astype(BF16) + high, low], axis=0)

    def send_columns(e, kind, ref):
        total = None
        for k, (f, _) in enumerate(kind["x"]):
            cells = ref[f, pl.ds(EDGE * rows, depth * rows), :]
            term = lax.dot_general(
                picker(k), cells.astype(BF16), (((1,), (1,)), ((), ())), preferred_element_type=F32
            )
            total = term if total is None else total + term
        grp_send[e] = total

    def columns_copy(e):
        return pltpu.make_async_remote_copy(
            src_ref=grp_send.at[e], dst_ref=grp_recv.at[e], send_sem=gsend_sem.at[e], recv_sem=grecv_sem.at[e],
            device_id=other, device_id_type=MESH,
        )

    def place_columns(e, kind):
        got = grp_recv[e].astype(BF16)
        pair = jnp.concatenate([got, got], axis=0)
        for k, (_, forward) in enumerate(kind["x"]):
            cross[k] = lax.dot_general(
                pair, placer(k, forward), (((0,), (0,)), ((), ())), preferred_element_type=F32
            )

    def row_at(ref, field, y):
        return ref.at[field, pl.ds(EDGE * rows + y, depth, stride=rows), :]

    def cell_row(ref, y):
        return ref.at[pl.ds(y, depth, stride=rows), :]

    def rows_copy(e, upward, count):
        src, dst = (up_send, up_recv) if upward else (dn_send, dn_recv)
        way = 0 if upward else 1
        return pltpu.make_async_remote_copy(
            src_ref=src.at[e, pl.ds(0, count)], dst_ref=dst.at[e, pl.ds(0, count)],
            send_sem=ysend_sem.at[e, way], recv_sem=yrecv_sem.at[e, way],
            device_id=next_y if upward else prev_y, device_id_type=MESH,
        )

    def planes_copies(e, kind, ref, upward):
        way = 0 if upward else 1
        copies = []
        for k, (f, forward) in enumerate(kind["z"]):
            count = 1 if forward == upward else 2
            first = EDGE + depth - count if upward else EDGE
            target = EDGE - count if upward else EDGE + depth
            copies.append(pltpu.make_async_remote_copy(
                src_ref=planes(ref, f, first, count),
                dst_ref=planes(ref, f, target, count),
                send_sem=zsend_sem.at[e, way, k], recv_sem=zrecv_sem.at[e, way, k],
                device_id=next_z if upward else prev_z, device_id_type=MESH,
            ))
        return copies

    kinds = (STRESS, MOTION) * STEPS
    refs = (s0, v1, s1, v2)

    def start_rows(e):
        kind = kinds[e]
        pl.when(has_next_y)(lambda: rows_copy(e, True, len(row_list(kind, True))).start())
        pl.when(has_prev_y)(lambda: rows_copy(e, False, len(row_list(kind, False))).start())

    def start_planes(e):
        for exists, upward in ((has_next_z, True), (has_prev_z, False)):
            @pl.when(exists)
            def _():
                for copy in planes_copies(e, kinds[e], refs[e], upward):
                    copy.start()

    def wait_planes(e):
        for exists, upward in ((has_prev_z, True), (has_next_z, False)):
            @pl.when(exists)
            def _():
                for copy in planes_copies(e, kinds[e], refs[e], upward):
                    copy.wait_recv()

    def wait_rows(e):
        kind = kinds[e]
        pl.when(has_prev_y)(lambda: rows_copy(e, True, len(row_list(kind, True))).wait_recv())
        pl.when(has_next_y)(lambda: rows_copy(e, False, len(row_list(kind, False))).wait_recv())

    def row_terms(e):
        kind = kinds[e]
        before, after = {}, {}
        for place, (k, _, far) in enumerate(row_list(kind, True)):
            before[k, far] = up_recv[e, place]
        for place, (k, _, far) in enumerate(row_list(kind, False)):
            after[k, far] = dn_recv[e, place]
        terms = []
        for k, (_, forward) in enumerate(kind["y"]):
            if forward:
                terms.append({
                    0: -RATIO * before[k, 0],
                    rows - 1: after[k, 0] + RATIO * after[k, 1],
                    rows - 2: RATIO * after[k, 0],
                })
            else:
                terms.append({
                    0: -before[k, 0] - RATIO * before[k, 1],
                    1: -RATIO * before[k, 0],
                    rows - 1: RATIO * after[k, 0],
                })
        return terms

    def fill_rows(e, values):
        kind, ref = kinds[e], refs[e]

        def value(field, y):
            got = values.get((field, y))
            return row_at(ref, field, y)[...] if got is None else got

        for place, (_, field, far) in enumerate(row_list(kind, True)):
            up_send[e, place] = value(field, rows - 1 - far)
        for place, (_, field, far) in enumerate(row_list(kind, False)):
            dn_send[e, place] = value(field, far)

    lane_id = lax.broadcasted_iota(jnp.int32, (rows, lanes), 1)
    row_id = lax.broadcasted_iota(jnp.int32, (rows, lanes), 0)

    def along_x(ref, field, p, forward):
        cells = ref[field, plane(p), :]
        one_back = jnp.where(lane_id >= 1, pltpu.roll(cells, 1, 1), 0.0)
        one_on = jnp.where(lane_id < lanes - 1, pltpu.roll(cells, lanes - 1, 1), 0.0)
        if forward:
            two_on = jnp.where(lane_id < lanes - 2, pltpu.roll(cells, lanes - 2, 1), 0.0)
            return one_on - cells, two_on - one_back
        two_back = jnp.where(lane_id >= 2, pltpu.roll(cells, 2, 1), 0.0)
        return cells - one_back, one_on - two_back

    def along_y(ref, field, p, forward):
        start = pl.multiple_of(p * rows, 8)

        def at(d):
            cells = ref[field, pl.ds(start + d, rows), :]
            if d == 0:
                return cells
            inside = row_id >= -d if d < 0 else row_id < rows - d
            return jnp.where(inside, cells, 0.0)

        if forward:
            return at(1) - at(0), at(2) - at(-1)
        return at(0) - at(-1), at(1) - at(-2)

    def along_z(ref, field, p, forward):
        at = lambda d: ref[field, plane(p + d), :]
        if forward:
            return at(1) - at(0), at(2) - at(-1)
        return at(0) - at(-1), at(1) - at(-2)

    def per_plane(ref, z):
        block = ref[z]
        return jnp.concatenate([block] * (rows // 8), axis=0)

    def inner(ref, z):
        return ref[plane(z), :]

    def joined(parts, extra):
        near = functools.reduce(lambda a, b: a + b, [n for n, _ in parts])
        far = functools.reduce(lambda a, b: a + b, [f for _, f in parts])
        total = near + RATIO * far
        return total if extra is None else total + extra

    def motion_plane(src, old, new, z):
        p = z + EDGE
        keep, weight = per_plane(keep_ref, z), inner(buoy, z)
        cases = (
            ((along_x, 0, True), (along_y, 1, False), (along_z, 2, False)),
            ((along_x, 1, False), (along_y, 3, True), (along_z, 4, False)),
            ((along_x, 2, False), (along_y, 4, False), (along_z, 5, True)),
        )
        for k, case in enumerate(cases):
            force = joined([way(src, f, p, fwd) for way, f, fwd in case], cross[k, plane(z), :])
            new[k, plane(p), :] = keep * old(k, z) + weight * force

    def tensor_plane(src, old, store, step, z):
        p = z + EDGE
        keep, lam_z, mu_z = per_plane(keep_ref, z), inner(lam, z), inner(mu, z)
        xx = joined([along_x(src, 0, p, False)], cross[0, plane(z), :])
        yy = joined([along_y(src, 1, p, False)], None)
        zz = joined([along_z(src, 2, p, False)], None)
        xy = joined([along_y(src, 0, p, True), along_x(src, 1, p, True)], cross[1, plane(z), :])
        xz = joined([along_z(src, 0, p, True), along_x(src, 2, p, True)], cross[2, plane(z), :])
        yz = joined([along_z(src, 1, p, True), along_y(src, 2, p, True)], None)
        spread = lam_z * (xx + yy + zz)
        twice = mu_z + mu_z
        store(0, z, keep * old(0, z) + (spread + twice * xx))
        store(1, z, keep * old(1, z) + mu_z * xy)
        store(2, z, keep * old(2, z) + mu_z * xz)
        store(3, z, keep * old(3, z) + (spread + twice * yy))
        store(4, z, keep * old(4, z) + mu_z * yz)
        store(5, z, keep * old(5, z) + (spread + twice * zz))
        strain[0, plane(z), :] = xy
        strain[1, plane(z), :] = yy
        strain[2, plane(z), :] = yz
        eout[6 * step + 0, plane(z), :] = (NEAR * xx).astype(BF16)
        eout[6 * step + 2, plane(z), :] = (0.5 * NEAR * xz).astype(BF16)
        eout[6 * step + 5, plane(z), :] = (NEAR * zz).astype(BF16)

    def planes_loop(body):
        def step(z, carry):
            body(z)
            return carry

        lax.fori_loop(0, depth, step, 0, unroll=2)

    outs = []

    def put(src, dst):
        copy = pltpu.make_async_copy(src, dst, out_sem.at[len(outs)])
        copy.start()
        outs.append(copy)

    for f in (1, 3, 4):
        stress_load[f].wait()
    fill_rows(0, {})
    for f in (0, 2):
        stress_load[f].wait()
    send_columns(0, STRESS, s0)
    stress_load[5].wait()

    neighbours = 1 + sum(e.astype(jnp.int32) for e in (has_prev_y, has_next_y, has_prev_z, has_next_z))
    pl.semaphore_wait(barrier, neighbours)
    start_rows(0)
    columns_copy(0).start()
    start_planes(0)

    for copy in (buoy_load, vel_load, lam_load, mu_load):
        copy.wait()

    def scale(z):
        gain = per_plane(gain_ref, z)
        for ref in (buoy, lam, mu):
            ref[plane(z), :] = gain * ref[plane(z), :]

    planes_loop(scale)

    def old_motion(ref):
        if ref is vin:
            return lambda k, z: vin[k, plane(z), :]
        return lambda k, z: ref[k, plane(z + EDGE), :]

    for step in range(STEPS):
        last = step == STEPS - 1
        e = 2 * step
        src, old, new = (s0, vin, v1) if step == 0 else (s1, v1, v2)
        columns_copy(e).wait_recv()
        place_columns(e, STRESS)
        wait_planes(e)
        planes_loop(functools.partial(motion_plane, src, old_motion(old), new))
        wait_rows(e)
        values = {}
        for k, terms in enumerate(row_terms(e)):
            for y, term in terms.items():
                got = row_at(new, k, y)[...] + cell_row(buoy, y)[...] * term
                row_at(new, k, y)[...] = got
                values[k, y] = got
        fill_rows(e + 1, values)
        start_rows(e + 1)
        start_planes(e + 1)
        send_columns(e + 1, MOTION, new)
        columns_copy(e + 1).start()
        if last:
            for k in range(3):
                put(interior(new, k), vout_hbm.at[k])

        e = e + 1
        src, old = (v1, s0) if step == 0 else (v2, s1)

        def old_tensor(f, z, ref=old):
            return ref[f, plane(z + EDGE), :]

        def store(f, z, value):
            if last:
                sfin[f, plane(z), :] = value
            else:
                s1[f, plane(z + EDGE), :] = value

        def tensor_row(f, y):
            return cell_row(sfin.at[f], y) if last else row_at(s1, f, y)

        columns_copy(e).wait_recv()
        place_columns(e, MOTION)
        wait_planes(e)
        planes_loop(functools.partial(tensor_plane, src, old_tensor, store, step))
        for f in (0, 2, 5):
            put(eout.at[6 * step + f], eout_hbm.at[step, f])
        if last:
            put(sfin.at[2], sout_hbm.at[2])
        wait_rows(e)
        values = {}

        def raise_row(f, y, amount):
            got = tensor_row(f, y)[...] + amount
            tensor_row(f, y)[...] = got
            values[f, y] = got

        for k, terms in enumerate(row_terms(e)):
            for y, term in terms.items():
                stored = cell_row(strain.at[k], y)
                stored[...] = stored[...] + term
                mu_row = cell_row(mu, y)[...]
                if k == 1:
                    spread = cell_row(lam, y)[...] * term
                    raise_row(0, y, spread)
                    raise_row(5, y, spread)
                    raise_row(3, y, spread + (mu_row + mu_row) * term)
                else:
                    raise_row(1 if k == 0 else 4, y, mu_row * term)
        if last:
            for f in (1, 4, 3, 0, 5):
                put(sfin.at[f], sout_hbm.at[f])
        else:
            fill_rows(e + 1, values)
            start_rows(e + 1)
            start_planes(e + 1)
            send_columns(e + 1, STRESS, s1)
            columns_copy(e + 1).start()

        def convert(z):
            for k, f, factor in ((0, 1, 0.5 * NEAR), (1, 3, NEAR), (2, 4, 0.5 * NEAR)):
                eout[6 * step + f, plane(z), :] = (factor * strain[k, plane(z), :]).astype(BF16)

        planes_loop(convert)
        for f in (1, 3, 4):
            put(eout.at[6 * step + f], eout_hbm.at[step, f])

    for e in range(2 * STEPS):
        kind = kinds[e]
        columns_copy(e).wait_send()
        pl.when(has_next_y)(lambda: rows_copy(e, True, len(row_list(kind, True))).wait_send())
        pl.when(has_prev_y)(lambda: rows_copy(e, False, len(row_list(kind, False))).wait_send())
        for exists, upward in ((has_next_z, True), (has_prev_z, False)):
            @pl.when(exists)
            def _():
                for copy in planes_copies(e, kinds[e], refs[e], upward):
                    copy.wait_send()
    for copy in outs:
        copy.wait()


def on_device(velocity, stress, buoyancy, lame_lambda, shear_modulus, pml_flag, profile_index, damping_peak):
    _, depth, rows, lanes = velocity.shape
    exchanges = 2 * STEPS
    cells = depth * rows
    any_spec = pl.BlockSpec(memory_space=pl.ANY)
    smem_spec = pl.BlockSpec(memory_space=pltpu.SMEM)
    dma = pltpu.SemaphoreType.DMA

    def fields(count):
        return pltpu.VMEM((count, (depth + 2 * EDGE) * rows, lanes), F32)

    vout, sout, eout = pl.pallas_call(
        functools.partial(kernel, depth, rows, lanes),
        out_shape=(
            jax.ShapeDtypeStruct((3, cells, lanes), F32),
            jax.ShapeDtypeStruct((6, cells, lanes), F32),
            jax.ShapeDtypeStruct((STEPS, 6, cells, lanes), BF16),
        ),
        in_specs=[any_spec] * 5 + [smem_spec] * 3,
        out_specs=(any_spec,) * 3,
        scratch_shapes=[
            fields(6),
            fields(6),
            fields(3),
            fields(3),
            pltpu.VMEM((6, cells, lanes), F32),
            pltpu.VMEM((3, cells, lanes), F32),
            pltpu.VMEM((cells, lanes), F32),
            pltpu.VMEM((cells, lanes), F32),
            pltpu.VMEM((cells, lanes), F32),
            pltpu.VMEM((depth, 8, lanes), F32),
            pltpu.VMEM((depth, 8, lanes), F32),
            pltpu.VMEM((3, cells, lanes), F32),
            pltpu.VMEM((3, cells, lanes), F32),
            pltpu.VMEM((6 * STEPS, cells, lanes), BF16),
            pltpu.VMEM((exchanges, 5, depth, lanes), F32),
            pltpu.VMEM((exchanges, 5, depth, lanes), F32),
            pltpu.VMEM((exchanges, 5, depth, lanes), F32),
            pltpu.VMEM((exchanges, 5, depth, lanes), F32),
            pltpu.VMEM((exchanges, 8, cells), F32),
            pltpu.VMEM((exchanges, 8, cells), F32),
            dma((10,)),
            dma((32,)),
            dma((exchanges, 2)),
            dma((exchanges, 2)),
            dma((exchanges, 2, 3)),
            dma((exchanges, 2, 3)),
            dma((exchanges,)),
            dma((exchanges,)),
        ],
        compiler_params=pltpu.CompilerParams(collective_id=0, has_side_effects=True),
        name="two_steps",
    )(
        velocity.reshape(3, cells, lanes),
        stress.reshape(6, cells, lanes),
        buoyancy.reshape(cells, lanes),
        lame_lambda.reshape(cells, lanes),
        shear_modulus.reshape(cells, lanes),
        pml_flag,
        profile_index,
        damping_peak,
    )
    return (
        vout.reshape(velocity.shape),
        sout.reshape(stress.shape),
        eout.reshape(STEPS, *stress.shape),
    )


def solution(mesh):
    return jax.shard_map(
        on_device,
        mesh=mesh,
        in_specs=(
            P(None, "gy", "gx", "grp"),
            P(None, "gy", "gx", "grp"),
            P("gy", "gx", "grp"),
            P("gy", "gx", "grp"),
            P("gy", "gx", "grp"),
            P("gy", "gx", "grp"),
            P("gy", "gx", "grp"),
            P(),
        ),
        out_specs=(
            P(None, "gy", "gx", "grp"),
            P(None, "gy", "gx", "grp"),
            P(None, None, "gy", "gx", "grp"),
        ),
        check_vma=False,
    )
```

time: 124 us -> 35.5 us (0.29)
  starting transfers between devices: 86.4 us -> 0 us
  Pallas kernels: 0 us -> 29.2 us
  waiting for transfers between devices: 18 us -> 0 us
  other arithmetic: 8.74 us -> 0 us
  local copies, waits for them, and re-layouts: 6.92 us -> 4.14 us
  between operations: 3.42 us -> 1.94 us
    ppermute x24 -> x0, starting transfers between devices: 86.4 us -> none  [the longest x12 54.1 us: extended(): before = lax.ppermute(last, axis, up)]
    pallas_call x0 -> x1, Pallas kernels: none -> 29.2 us  [on_device(): pl.pallas_call(functools.partial(kernel, depth, rows, lanes), out_shape=(...]
    ppermute x24 -> x0, waiting for transfers between devices: 18 us -> none  [the longest x12 15.8 us: extended(): before = lax.ppermute(last, axis, up)]
    slice x13 -> x0, local copies, waits for them, and re-layouts: 3.86 us -> none  [the longest x3 1.97 us: tensor_pads(): grouped = extended(stress[:3].astype(jnp.bfloat16), (('grp', 3),), 2)]
    unnamed x20 -> x0, other arithmetic: 2.74 us -> none
    another operation x9 -> x0, other arithmetic: 2.03 us -> none  [the longest x1 1.01 us: on_device(): return (velocity, stress, jnp.stack(strain_steps))]
    concatenate x8 -> x0, other arithmetic: 1.84 us -> none  [the longest x4 1.48 us: join_group(): jnp.concatenate([grouped[..., :2].astype(jnp.float32), local, grouped[......]
    unnamed x16 -> x7, local copies, waits for them, and re-layouts: 2.74 us -> 4.14 us
  transfers between devices with their start and end apart: 24 -> 0, of which waited for: 10 -> 0; matrix products, arithmetic and copies ran while one was open for 4% -> 0% of each run, Pallas kernels for 0% -> 0%
where the time goes in v1:
time: 35.5 us; the launch traced here: 35.2 us
  Pallas kernels  29.2 us (82%)
  local copies, waits for them, and re-layouts  4.14 us (12%)
  between operations  1.94 us (5%)
    pallas_call x1, Pallas kernels, on_device(): pl.pallas_call(functools.partial(kernel, depth, rows, lanes), out_shape=(...  29.2 us
    unnamed x7, local copies, waits for them, and re-layouts  4.14 us

profile of v1, /device:TPU:199, one launch (start us, length us, event | category | flops | bytes accessed | tf_op | source)
XLA Modules:
  0.0 35.2 jit_solution(4118727478992320349)
XLA Ops:
  1.9 29.2 %two_steps.1 = (f32[3,256,128]{2,1,0:T(8,128)}, f32[6,256,128]{2,1,0:T(8,128)}, bf16[2,6,256,128]{3,2,1,0:T(8,128)(2,1)}) custom-call(f32[3,256,128]{2,1,0:T(8,128)} %bitcast.12, f32[6,256,128]{2,1,0:T(8,128)} %bitcast.8, f32[256,128]{1,0:T(8,128)} %bitcast.13, f32[256,128]{1,0:T(8,128)} %bitcast.14, f32[256,128]{1,0:T(8,128)} %bitcast.15, ...), custom_call_target="tpu_custom_call" | custom-call | tf_op jit(solution)/shard_map/two_steps/pallas_call | solution.py:502
  31.1 0.0 copy-start.1
  31.1 1.8 %copy.16 = f32[3,16,16,128]{3,2,1,0:T(8,128)} copy(f32[3,16,16,128]{3,2,1,0:T(8,128)} %bitcast.11) | data formatting | bytes 786432
  32.9 0.0 copy-done.1
  33.0 0.0 copy-start
  33.0 0.9 %copy.17 = f32[6,16,16,128]{3,2,1,0:T(8,128)} copy(f32[6,16,16,128]{3,2,1,0:T(8,128)S(1)} %bitcast.10) | data formatting | bytes 1572864
  33.8 0.5 %copy-done = bf16[2,6,256,128]{3,2,1,0:T(8,128)(2,1)S(1)} copy-done((bf16[2,6,256,128]{3,2,1,0:T(8,128)(2,1)S(1)}, bf16[2,6,256,128]{3,2,1,0:T(8,128)(2,1)}, u32[]{:S(2)}) %copy-start) | copy-done | bytes 786456
  34.4 0.9 %copy.18 = bf16[2,6,16,16,128]{4,3,2,1,0:T(8,128)(2,1)} copy(bf16[2,6,16,16,128]{4,3,2,1,0:T(8,128)(2,1)S(1)} %bitcast.9) | data formatting | bytes 1572864
Async XLA Ops:
  31.1 1.9 %copy-start.1 = (f32[6,256,128]{2,1,0:T(8,128)S(1)}, f32[6,256,128]{2,1,0:T(8,128)}, u32[]{:S(2)}) copy-start(f32[6,256,128]{2,1,0:T(8,128)} %get-tuple-element.7) | copy-start | bytes 2359300
  33.0 1.4 %copy-start = (bf16[2,6,256,128]{3,2,1,0:T(8,128)(2,1)S(1)}, bf16[2,6,256,128]{3,2,1,0:T(8,128)(2,1)}, u32[]{:S(2)}) copy-start(bf16[2,6,256,128]{3,2,1,0:T(8,128)(2,1)} %get-tuple-element.8) | copy-start | bytes 2359300

commit v2 on v1

--- a/solution.py
+++ b/solution.py
@@ -18,6 +18,8 @@
 HALF = 0.5 * TIME_STEP
 
 EDGE = 2
+
+VMEM_LIMIT = 24 * 1024 * 1024
 
 STRESS = {
     "x": ((0, True), (1, False), (2, False)),
@@ -31,23 +33,46 @@
 }
 
 
+STRAIN = {"x": (0, 1, 2), "y": (1, 3, 4), "z": (2, 4, 5)}
+NORMAL = (0, 3, 5)
+
+
 def row_list(kind, upward):
-    rows = []
-    for slot, (field, forward) in enumerate(kind["y"]):
-        rows.append((slot, field, 0))
-    for slot, (field, forward) in enumerate(kind["y"]):
-        if forward != upward:
-            rows.append((slot, field, 1))
+    rows = [(slot, field, 0) for slot, (field, forward) in enumerate(kind["y"])]
+    rows += [(slot, field, 1) for slot, (field, forward) in enumerate(kind["y"]) if forward != upward]
     return rows
+
+
+def plane_list(kind, upward):
+    runs, place = [], 0
+    for field, forward in kind["z"]:
+        count = 1 if forward == upward else 2
+        runs.append((field, count, place))
+        place += count
+    return runs
+
+
+def halo_terms(forward, before, after, length):
+    if forward:
+        return {
+            0: -RATIO * before[0],
+            length - 1: after[0] + RATIO * after[1],
+            length - 2: RATIO * after[0],
+        }
+    return {
+        0: -before[0] - RATIO * before[1],
+        1: -RATIO * before[0],
+        length - 1: RATIO * after[0],
+    }
 
 
 def kernel(
     depth, rows, lanes,
-    vel_hbm, str_hbm, buoy_hbm, lam_hbm, mu_hbm, flag_ref, prof_ref, peak_ref,
-    vout_hbm, sout_hbm, eout_hbm,
-    s0, s1, v1, v2, sfin, vin, buoy, lam, mu, keep_ref, gain_ref, cross, strain, eout,
-    up_send, up_recv, dn_send, dn_recv, grp_send, grp_recv,
-    in_sem, out_sem, ysend_sem, yrecv_sem, zsend_sem, zrecv_sem, gsend_sem, grecv_sem,
+    vel_hbm, str_hbm, buoy_hbm, lam_hbm, mu_hbm, peak_hbm, flag_ref, prof_ref,
+    v2, sfin, eout,
+    s0, s1, v1, vin, buoy, lam, mu, keep_ref, gain_ref, strain, peak_ref,
+    up_send, up_recv, dn_send, dn_recv, zup_recv, zdn_recv, grp_send, grp_recv,
+    in_sem, ysend_sem, yrecv_sem, zsend_sem, zrecv_sem, gsend_sem, grecv_sem,
 ):
     gx, gy, grp = lax.axis_index("gx"), lax.axis_index("gy"), lax.axis_index("grp")
     n_gx, n_gy = lax.axis_size("gx"), lax.axis_size("gy")
@@ -90,37 +115,34 @@
     vel_load = load(vel_hbm, vin)
     lam_load = load(lam_hbm, lam)
     mu_load = load(mu_hbm, mu)
-
-    z_fields = ((s0, (2, 4, 5)), (s1, (2, 4, 5)), (v1, (0, 1, 2)), (v2, (0, 1, 2)))
-
-    def clear_planes(first):
-        for ref, fields in z_fields:
-            for f in fields:
+    peak_load = load(peak_hbm, peak_ref)
+
+    for ref, fields in ((s0, (2, 4, 5)), (s1, (2, 4, 5)), (v1, (0, 1, 2)), (v2, (0, 1, 2))):
+        for f in fields:
+            for first in (0, EDGE + depth):
                 ref[f, pl.ds(first * rows, EDGE * rows), :] = jnp.zeros((EDGE * rows, lanes), F32)
 
-    pl.when(jnp.logical_not(has_prev_z))(functools.partial(clear_planes, 0))
-    pl.when(jnp.logical_not(has_next_z))(functools.partial(clear_planes, EDGE + depth))
-
-    def clear_recv(ref):
-        ref[...] = jnp.zeros_like(ref)
+    def clear_recv(*refs):
+        for ref in refs:
+            ref[...] = jnp.zeros_like(ref)
 
     pl.when(jnp.logical_not(has_prev_y))(functools.partial(clear_recv, up_recv))
     pl.when(jnp.logical_not(has_next_y))(functools.partial(clear_recv, dn_recv))
-
-    choice = prof_ref[0, 0, 0]
-    peak = jnp.float32(0.0)
-    for i in range(peak_ref.shape[0]):
-        peak = peak + jnp.where(choice == i, peak_ref[i], 0.0)
-    rate = flag_ref[0, 0, 0].astype(F32) * peak
-
-    def damping_of(shape):
-        z = (lax.broadcasted_iota(jnp.int32, shape, 0) + gy * depth).astype(F32)
+    pl.when(jnp.logical_not(has_prev_z))(functools.partial(clear_recv, zup_recv))
+    pl.when(jnp.logical_not(has_next_z))(functools.partial(clear_recv, zdn_recv))
+
+    def set_damping():
+        choice = prof_ref[0, 0, 0]
+        peak = jnp.float32(0.0)
+        for i in range(peak_ref.shape[0]):
+            peak = peak + jnp.where(choice == i, peak_ref[i], 0.0)
+        rate = flag_ref[0, 0, 0].astype(F32) * peak
+        z = (lax.broadcasted_iota(jnp.int32, (depth, 8, lanes), 0) + gy * depth).astype(F32)
         q = (z + 0.5) / (depth * n_gy)
         damping = rate * (0.5 + 0.5 * q * q)
         divide = 1.0 + HALF * damping
-        return (1.0 - HALF * damping) / divide, (NEAR * TIME_STEP) / divide
-
-    keep_ref[...], gain_ref[...] = damping_of((depth, 8, lanes))
+        keep_ref[...] = (1.0 - HALF * damping) / divide
+        gain_ref[...] = (NEAR * TIME_STEP) / divide
 
     slot = lax.broadcasted_iota(jnp.int32, (8, lanes), 0)
     lane = lax.broadcasted_iota(jnp.int32, (8, lanes), 1)
@@ -164,13 +186,13 @@
             device_id=other, device_id_type=MESH,
         )
 
-    def place_columns(e, kind):
+    def column_terms(e):
         got = grp_recv[e].astype(BF16)
         pair = jnp.concatenate([got, got], axis=0)
-        for k, (_, forward) in enumerate(kind["x"]):
-            cross[k] = lax.dot_general(
-                pair, placer(k, forward), (((0,), (0,)), ((), ())), preferred_element_type=F32
-            )
+        return [
+            lax.dot_general(pair, placer(k, forward), (((0,), (0,)), ((), ())), preferred_element_type=F32)
+            for k, (_, forward) in enumerate(kinds[e]["x"])
+        ]
 
     def row_at(ref, field, y):
         return ref.at[field, pl.ds(EDGE * rows + y, depth, stride=rows), :]
@@ -187,16 +209,14 @@
             device_id=next_y if upward else prev_y, device_id_type=MESH,
         )
 
-    def planes_copies(e, kind, ref, upward):
-        way = 0 if upward else 1
+    def planes_copies(e, upward):
+        way, dst = (0, zup_recv) if upward else (1, zdn_recv)
         copies = []
-        for k, (f, forward) in enumerate(kind["z"]):
-            count = 1 if forward == upward else 2
+        for k, (f, count, place) in enumerate(plane_list(kinds[e], upward)):
             first = EDGE + depth - count if upward else EDGE
-            target = EDGE - count if upward else EDGE + depth
             copies.append(pltpu.make_async_remote_copy(
-                src_ref=planes(ref, f, first, count),
-                dst_ref=planes(ref, f, target, count),
+                src_ref=planes(refs[e], f, first, count),
+                dst_ref=dst.at[e, pl.ds(place * rows, count * rows), :],
                 send_sem=zsend_sem.at[e, way, k], recv_sem=zrecv_sem.at[e, way, k],
                 device_id=next_z if upward else prev_z, device_id_type=MESH,
             ))
@@ -214,14 +234,14 @@
         for exists, upward in ((has_next_z, True), (has_prev_z, False)):
             @pl.when(exists)
             def _():
-                for copy in planes_copies(e, kinds[e], refs[e], upward):
+                for copy in planes_copies(e, upward):
                     copy.start()
 
     def wait_planes(e):
         for exists, upward in ((has_prev_z, True), (has_next_z, False)):
             @pl.when(exists)
             def _():
-                for copy in planes_copies(e, kinds[e], refs[e], upward):
+                for copy in planes_copies(e, upward):
                     copy.wait_recv()
 
     def wait_rows(e):
@@ -231,25 +251,28 @@
 
     def row_terms(e):
         kind = kinds[e]
-        before, after = {}, {}
-        for place, (k, _, far) in enumerate(row_list(kind, True)):
-            before[k, far] = up_recv[e, place]
-        for place, (k, _, far) in enumerate(row_list(kind, False)):
-            after[k, far] = dn_recv[e, place]
+        before = {(k, far): up_recv[e, place] for place, (k, _, far) in enumerate(row_list(kind, True))}
+        after = {(k, far): dn_recv[e, place] for place, (k, _, far) in enumerate(row_list(kind, False))}
+        return [
+            halo_terms(
+                forward,
+                [before[k, far] for far in range(2) if (k, far) in before],
+                [after[k, far] for far in range(2) if (k, far) in after],
+                rows,
+            )
+            for k, (_, forward) in enumerate(kind["y"])
+        ]
+
+    def plane_terms(e):
+        kind = kinds[e]
         terms = []
-        for k, (_, forward) in enumerate(kind["y"]):
-            if forward:
-                terms.append({
-                    0: -RATIO * before[k, 0],
-                    rows - 1: after[k, 0] + RATIO * after[k, 1],
-                    rows - 2: RATIO * after[k, 0],
-                })
-            else:
-                terms.append({
-                    0: -before[k, 0] - RATIO * before[k, 1],
-                    1: -RATIO * before[k, 0],
-                    rows - 1: RATIO * after[k, 0],
-                })
+        for k, (_, forward) in enumerate(kind["z"]):
+            layers = []
+            for upward, ref in ((True, zup_recv), (False, zdn_recv)):
+                _, count, place = plane_list(kind, upward)[k]
+                got = [ref[e, pl.ds((place + i) * rows, rows), :] for i in range(count)]
+                layers.append(got[::-1] if upward else got)
+            terms.append(halo_terms(forward, *layers, depth))
         return terms
 
     def fill_rows(e, values):
@@ -304,11 +327,10 @@
     def inner(ref, z):
         return ref[plane(z), :]
 
-    def joined(parts, extra):
+    def joined(*parts):
         near = functools.reduce(lambda a, b: a + b, [n for n, _ in parts])
         far = functools.reduce(lambda a, b: a + b, [f for _, f in parts])
-        total = near + RATIO * far
-        return total if extra is None else total + extra
+        return near + RATIO * far
 
     def motion_plane(src, old, new, z):
         p = z + EDGE
@@ -319,18 +341,18 @@
             ((along_x, 2, False), (along_y, 4, False), (along_z, 5, True)),
         )
         for k, case in enumerate(cases):
-            force = joined([way(src, f, p, fwd) for way, f, fwd in case], cross[k, plane(z), :])
+            force = joined(*[way(src, f, p, fwd) for way, f, fwd in case])
             new[k, plane(p), :] = keep * old(k, z) + weight * force
 
-    def tensor_plane(src, old, store, step, z):
+    def tensor_plane(src, old, store, z):
         p = z + EDGE
         keep, lam_z, mu_z = per_plane(keep_ref, z), inner(lam, z), inner(mu, z)
-        xx = joined([along_x(src, 0, p, False)], cross[0, plane(z), :])
-        yy = joined([along_y(src, 1, p, False)], None)
-        zz = joined([along_z(src, 2, p, False)], None)
-        xy = joined([along_y(src, 0, p, True), along_x(src, 1, p, True)], cross[1, plane(z), :])
-        xz = joined([along_z(src, 0, p, True), along_x(src, 2, p, True)], cross[2, plane(z), :])
-        yz = joined([along_z(src, 1, p, True), along_y(src, 2, p, True)], None)
+        xx = joined(along_x(src, 0, p, False))
+        yy = joined(along_y(src, 1, p, False))
+        zz = joined(along_z(src, 2, p, False))
+        xy = joined(along_y(src, 0, p, True), along_x(src, 1, p, True))
+        xz = joined(along_z(src, 0, p, True), along_x(src, 2, p, True))
+        yz = joined(along_z(src, 1, p, True), along_y(src, 2, p, True))
         spread = lam_z * (xx + yy + zz)
         twice = mu_z + mu_z
         store(0, z, keep * old(0, z) + (spread + twice * xx))
@@ -339,12 +361,8 @@
         store(3, z, keep * old(3, z) + (spread + twice * yy))
         store(4, z, keep * old(4, z) + mu_z * yz)
         store(5, z, keep * old(5, z) + (spread + twice * zz))
-        strain[0, plane(z), :] = xy
-        strain[1, plane(z), :] = yy
-        strain[2, plane(z), :] = yz
-        eout[6 * step + 0, plane(z), :] = (NEAR * xx).astype(BF16)
-        eout[6 * step + 2, plane(z), :] = (0.5 * NEAR * xz).astype(BF16)
-        eout[6 * step + 5, plane(z), :] = (NEAR * zz).astype(BF16)
+        for f, value in enumerate((xx, xy, xz, yy, yz, zz)):
+            strain[f, plane(z), :] = value
 
     def planes_loop(body):
         def step(z, carry):
@@ -352,13 +370,6 @@
             return carry
 
         lax.fori_loop(0, depth, step, 0, unroll=2)
-
-    outs = []
-
-    def put(src, dst):
-        copy = pltpu.make_async_copy(src, dst, out_sem.at[len(outs)])
-        copy.start()
-        outs.append(copy)
 
     for f in (1, 3, 4):
         stress_load[f].wait()
@@ -374,8 +385,9 @@
     columns_copy(0).start()
     start_planes(0)
 
-    for copy in (buoy_load, vel_load, lam_load, mu_load):
+    for copy in (peak_load, buoy_load, vel_load, lam_load, mu_load):
         copy.wait()
+    set_damping()
 
     def scale(z):
         gain = per_plane(gain_ref, z)
@@ -393,10 +405,16 @@
         last = step == STEPS - 1
         e = 2 * step
         src, old, new = (s0, vin, v1) if step == 0 else (s1, v1, v2)
+        planes_loop(functools.partial(motion_plane, src, old_motion(old), new))
+        wait_planes(e)
+        for k, terms in enumerate(plane_terms(e)):
+            for z, term in terms.items():
+                cells = new.at[k, pl.ds((z + EDGE) * rows, rows), :]
+                cells[...] = cells[...] + buoy[pl.ds(z * rows, rows), :] * term
         columns_copy(e).wait_recv()
-        place_columns(e, STRESS)
-        wait_planes(e)
-        planes_loop(functools.partial(motion_plane, src, old_motion(old), new))
+        for k, term in enumerate(column_terms(e)):
+            cells = interior(new, k)
+            cells[...] = cells[...] + buoy[...] * term
         wait_rows(e)
         values = {}
         for k, terms in enumerate(row_terms(e)):
@@ -409,9 +427,6 @@
         start_planes(e + 1)
         send_columns(e + 1, MOTION, new)
         columns_copy(e + 1).start()
-        if last:
-            for k in range(3):
-                put(interior(new, k), vout_hbm.at[k])
 
         e = e + 1
         src, old = (v1, s0) if step == 0 else (v2, s1)
@@ -425,54 +440,72 @@
             else:
                 s1[f, plane(z + EDGE), :] = value
 
-        def tensor_row(f, y):
-            return cell_row(sfin.at[f], y) if last else row_at(s1, f, y)
-
+        def correct(component, term, stress_at, cell_at, strain_at):
+            changed = {}
+            place = strain_at(component)
+            place[...] = place[...] + term
+            shear = cell_at(mu)[...] * term
+            if component in NORMAL:
+                spread = cell_at(lam)[...] * term
+                for f in NORMAL:
+                    changed[f] = spread + (shear + shear) if f == component else spread
+            else:
+                changed[component] = shear
+            for f, amount in changed.items():
+                changed[f] = stress_at(f)[...] + amount
+                stress_at(f)[...] = changed[f]
+            return changed
+
+        def convert(components):
+            def body(z):
+                for f in components:
+                    factor = NEAR if f in NORMAL else 0.5 * NEAR
+                    eout[6 * step + f, plane(z), :] = (factor * strain[f, plane(z), :]).astype(BF16)
+
+            planes_loop(body)
+
+        planes_loop(functools.partial(tensor_plane, src, old_tensor, store))
+        wait_planes(e)
+        for k, terms in enumerate(plane_terms(e)):
+            for z, term in terms.items():
+                cell = pl.ds(z * rows, rows)
+                correct(
+                    STRAIN["z"][k], term,
+                    lambda f: sfin.at[f, cell, :] if last else s1.at[f, pl.ds((z + EDGE) * rows, rows), :],
+                    lambda ref: ref.at[cell, :],
+                    lambda f: strain.at[f, cell, :],
+                )
         columns_copy(e).wait_recv()
-        place_columns(e, MOTION)
-        wait_planes(e)
-        planes_loop(functools.partial(tensor_plane, src, old_tensor, store, step))
-        for f in (0, 2, 5):
-            put(eout.at[6 * step + f], eout_hbm.at[step, f])
+        for k, term in enumerate(column_terms(e)):
+            correct(
+                STRAIN["x"][k], term,
+                lambda f: sfin.at[f] if last else interior(s1, f),
+                lambda ref: ref,
+                lambda f: strain.at[f],
+            )
         if last:
-            put(sfin.at[2], sout_hbm.at[2])
+            convert((0, 2, 5))
         wait_rows(e)
         values = {}
-
-        def raise_row(f, y, amount):
-            got = tensor_row(f, y)[...] + amount
-            tensor_row(f, y)[...] = got
-            values[f, y] = got
-
         for k, terms in enumerate(row_terms(e)):
             for y, term in terms.items():
-                stored = cell_row(strain.at[k], y)
-                stored[...] = stored[...] + term
-                mu_row = cell_row(mu, y)[...]
-                if k == 1:
-                    spread = cell_row(lam, y)[...] * term
-                    raise_row(0, y, spread)
-                    raise_row(5, y, spread)
-                    raise_row(3, y, spread + (mu_row + mu_row) * term)
-                else:
-                    raise_row(1 if k == 0 else 4, y, mu_row * term)
+                changed = correct(
+                    STRAIN["y"][k], term,
+                    lambda f: cell_row(sfin.at[f], y) if last else row_at(s1, f, y),
+                    lambda ref: cell_row(ref, y),
+                    lambda f: cell_row(strain.at[f], y),
+                )
+                for f, got in changed.items():
+                    values[f, y] = got
         if last:
-            for f in (1, 4, 3, 0, 5):
-                put(sfin.at[f], sout_hbm.at[f])
+            convert((1, 3, 4))
         else:
             fill_rows(e + 1, values)
             start_rows(e + 1)
             start_planes(e + 1)
             send_columns(e + 1, STRESS, s1)
             columns_copy(e + 1).start()
-
-        def convert(z):
-            for k, f, factor in ((0, 1, 0.5 * NEAR), (1, 3, NEAR), (2, 4, 0.5 * NEAR)):
-                eout[6 * step + f, plane(z), :] = (factor * strain[k, plane(z), :]).astype(BF16)
-
-        planes_loop(convert)
-        for f in (1, 3, 4):
-            put(eout.at[6 * step + f], eout_hbm.at[step, f])
+            convert(range(6))
 
     for e in range(2 * STEPS):
         kind = kinds[e]
@@ -482,9 +515,26 @@
         for exists, upward in ((has_next_z, True), (has_prev_z, False)):
             @pl.when(exists)
             def _():
-                for copy in planes_copies(e, kinds[e], refs[e], upward):
+                for copy in planes_copies(e, upward):
                     copy.wait_send()
-    for copy in outs:
+
+
+def write_out(v2, sfin, eout, vout_hbm, sout_hbm, eout_hbm, sem):
+    cells = vout_hbm.shape[1]
+    edge = (v2.shape[1] - cells) // 2
+    copies = []
+
+    def put(src, dst):
+        copies.append(pltpu.make_async_copy(src, dst, sem.at[len(copies)]))
+        copies[-1].start()
+
+    for f in range(6):
+        put(sfin.at[f], sout_hbm.at[f])
+    for f in range(3):
+        put(v2.at[f, pl.ds(edge, cells), :], vout_hbm.at[f])
+    for f in range(6 * STEPS):
+        put(eout.at[f], eout_hbm.at[f])
+    for copy in copies:
         copy.wait()
 
 
@@ -493,44 +543,43 @@
     exchanges = 2 * STEPS
     cells = depth * rows
     any_spec = pl.BlockSpec(memory_space=pl.ANY)
-    smem_spec = pl.BlockSpec(memory_space=pltpu.SMEM)
+    vmem_spec = pl.BlockSpec(memory_space=pltpu.VMEM)
     dma = pltpu.SemaphoreType.DMA
+    halo_cells = (depth + 2 * EDGE) * rows
 
     def fields(count):
-        return pltpu.VMEM((count, (depth + 2 * EDGE) * rows, lanes), F32)
-
-    vout, sout, eout = pl.pallas_call(
+        return pltpu.VMEM((count, halo_cells, lanes), F32)
+
+    final = pl.pallas_call(
         functools.partial(kernel, depth, rows, lanes),
         out_shape=(
-            jax.ShapeDtypeStruct((3, cells, lanes), F32),
+            jax.ShapeDtypeStruct((3, halo_cells, lanes), F32),
             jax.ShapeDtypeStruct((6, cells, lanes), F32),
-            jax.ShapeDtypeStruct((STEPS, 6, cells, lanes), BF16),
+            jax.ShapeDtypeStruct((6 * STEPS, cells, lanes), BF16),
         ),
-        in_specs=[any_spec] * 5 + [smem_spec] * 3,
-        out_specs=(any_spec,) * 3,
+        in_specs=[any_spec] * 6 + [pl.BlockSpec(memory_space=pltpu.SMEM)] * 2,
+        out_specs=(vmem_spec,) * 3,
         scratch_shapes=[
             fields(6),
             fields(6),
             fields(3),
-            fields(3),
-            pltpu.VMEM((6, cells, lanes), F32),
             pltpu.VMEM((3, cells, lanes), F32),
             pltpu.VMEM((cells, lanes), F32),
             pltpu.VMEM((cells, lanes), F32),
             pltpu.VMEM((cells, lanes), F32),
             pltpu.VMEM((depth, 8, lanes), F32),
             pltpu.VMEM((depth, 8, lanes), F32),
-            pltpu.VMEM((3, cells, lanes), F32),
-            pltpu.VMEM((3, cells, lanes), F32),
-            pltpu.VMEM((6 * STEPS, cells, lanes), BF16),
+            pltpu.VMEM((6, cells, lanes), F32),
+            pltpu.SMEM(damping_peak.shape, F32),
             pltpu.VMEM((exchanges, 5, depth, lanes), F32),
             pltpu.VMEM((exchanges, 5, depth, lanes), F32),
             pltpu.VMEM((exchanges, 5, depth, lanes), F32),
             pltpu.VMEM((exchanges, 5, depth, lanes), F32),
+            pltpu.VMEM((exchanges, 5 * rows, lanes), F32),
+            pltpu.VMEM((exchanges, 5 * rows, lanes), F32),
             pltpu.VMEM((exchanges, 8, cells), F32),
             pltpu.VMEM((exchanges, 8, cells), F32),
-            dma((10,)),
-            dma((32,)),
+            dma((11,)),
             dma((exchanges, 2)),
             dma((exchanges, 2)),
             dma((exchanges, 2, 3)),
@@ -538,18 +587,38 @@
             dma((exchanges,)),
             dma((exchanges,)),
         ],
-        compiler_params=pltpu.CompilerParams(collective_id=0, has_side_effects=True),
+        compiler_params=pltpu.CompilerParams(
+            collective_id=0, has_side_effects=True, vmem_limit_bytes=VMEM_LIMIT
+        ),
         name="two_steps",
     )(
-        velocity.reshape(3, cells, lanes),
-        stress.reshape(6, cells, lanes),
-        buoyancy.reshape(cells, lanes),
-        lame_lambda.reshape(cells, lanes),
-        shear_modulus.reshape(cells, lanes),
+        *[
+            pltpu.with_memory_space_constraint(x, pltpu.HBM)
+            for x in (
+                velocity.reshape(3, cells, lanes),
+                stress.reshape(6, cells, lanes),
+                buoyancy.reshape(cells, lanes),
+                lame_lambda.reshape(cells, lanes),
+                shear_modulus.reshape(cells, lanes),
+                damping_peak,
+            )
+        ],
         pml_flag,
         profile_index,
-        damping_peak,
     )
+    vout, sout, eout = pl.pallas_call(
+        write_out,
+        out_shape=(
+            jax.ShapeDtypeStruct((3, cells, lanes), F32),
+            jax.ShapeDtypeStruct((6, cells, lanes), F32),
+            jax.ShapeDtypeStruct((6 * STEPS, cells, lanes), BF16),
+        ),
+        in_specs=[any_spec] * 3,
+        out_specs=(any_spec,) * 3,
+        scratch_shapes=[dma((9 + 6 * STEPS,))],
+        compiler_params=pltpu.CompilerParams(vmem_limit_bytes=VMEM_LIMIT),
+        name="write_out",
+    )(*final)
     return (
         vout.reshape(velocity.shape),
         sout.reshape(stress.shape),

time: 35.5 us -> 30 us (0.85)
  local copies, waits for them, and re-layouts: 4.14 us -> 0 us
  Pallas kernels: 29.2 us -> 27.9 us
    unnamed x7 -> x0, local copies, waits for them, and re-layouts: 4.14 us -> none
    pallas_call x1, Pallas kernels: 29.2 us -> 26.5 us  [on_device(): pl.pallas_call(functools.partial(kernel, depth, rows, lanes), out_shape=(...]
    pallas_call x0 -> x1, Pallas kernels: none -> 1.44 us  [on_device(): pl.pallas_call(write_out, out_shape=(jax.ShapeDtypeStruct((3, cells, lane...]
where the time goes in v2:
time: 30 us; the launch traced here: 29.8 us
  Pallas kernels  27.9 us (93%)
  between operations  1.93 us (6%)
    pallas_call x1, Pallas kernels, on_device(): pl.pallas_call(functools.partial(kernel, depth, rows, lanes), out_shape=(...  26.5 us
    pallas_call x1, Pallas kernels, on_device(): pl.pallas_call(write_out, out_shape=(jax.ShapeDtypeStruct((3, cells, lane...  1.44 us

profile of v2, /device:TPU:199, one launch (start us, length us, event | category | flops | bytes accessed | tf_op | source)
XLA Modules:
  0.0 29.8 jit_solution(2998280609444097436)
XLA Ops:
  1.9 26.5 %two_steps.1 = (f32[3,320,128]{2,1,0:T(8,128)S(1)}, f32[6,256,128]{2,1,0:T(8,128)S(1)}, bf16[12,256,128]{2,1,0:T(8,128)(2,1)S(1)}) custom-call(f32[3,256,128]{2,1,0:T(8,128)} %bitcast.9, f32[6,256,128]{2,1,0:T(8,128)} %bitcast.8, f32[256,128]{1,0:T(8,128)} %bitcast.10, f32[256,128]{1,0:T(8,128)} %bitcast.11, f32[256,128]{1,0:T(8,128)} %bitcast.12, ...), custom_call_target="tpu_custom_call" | custom-call | tf_op jit(solution)/shard_map/two_steps/pallas_call | solution.py:553
  28.4 1.4 %write_out.1 = (f32[3,256,128]{2,1,0:T(8,128)}, f32[6,256,128]{2,1,0:T(8,128)}, bf16[12,256,128]{2,1,0:T(8,128)(2,1)}) custom-call(f32[3,320,128]{2,1,0:T(8,128)S(1)} %get-tuple-element.9.v2, f32[6,256,128]{2,1,0:T(8,128)S(1)} %get-tuple-element.10.sfin, bf16[12,256,128]{2,1,0:T(8,128)(2,1)S(1)} %get-tuple-element.11.eout), custom_call_target="tpu_custom_call" | custom-call | tf_op jit(solution)/shard_map/write_out/pallas_call | solution.py:609

commit v3 on v2

--- a/solution.py
+++ b/solution.py
@@ -37,19 +37,12 @@
 NORMAL = (0, 3, 5)
 
 
-def row_list(kind, upward):
-    rows = [(slot, field, 0) for slot, (field, forward) in enumerate(kind["y"])]
-    rows += [(slot, field, 1) for slot, (field, forward) in enumerate(kind["y"]) if forward != upward]
-    return rows
-
-
-def plane_list(kind, upward):
-    runs, place = [], 0
-    for field, forward in kind["z"]:
-        count = 1 if forward == upward else 2
-        runs.append((field, count, place))
-        place += count
-    return runs
+def whole_list(fields, upward):
+    return [k for k, (_, forward) in enumerate(fields) if forward != upward]
+
+
+def part_depth(forward, upward):
+    return 1 if forward != upward else 0
 
 
 def halo_terms(forward, before, after, length):
@@ -71,7 +64,8 @@
     vel_hbm, str_hbm, buoy_hbm, lam_hbm, mu_hbm, peak_hbm, flag_ref, prof_ref,
     v2, sfin, eout,
     s0, s1, v1, vin, buoy, lam, mu, keep_ref, gain_ref, strain, peak_ref,
-    up_send, up_recv, dn_send, dn_recv, zup_recv, zdn_recv, grp_send, grp_recv,
+    ywhole_send, ywhole_recv, ypart_send, ypart_recv, zwhole_send, zwhole_recv, zpart_send, zpart_recv,
+    grp_send, grp_recv,
     in_sem, ysend_sem, yrecv_sem, zsend_sem, zrecv_sem, gsend_sem, grecv_sem,
 ):
     gx, gy, grp = lax.axis_index("gx"), lax.axis_index("gy"), lax.axis_index("grp")
@@ -110,7 +104,7 @@
         loads.append(copy)
         return copy
 
-    stress_load = {f: load(str_hbm.at[f], interior(s0, f)) for f in (1, 3, 4, 0, 2, 5)}
+    stress_load = {f: load(str_hbm.at[f], interior(s0, f)) for f in (1, 3, 4, 2, 5, 0)}
     buoy_load = load(buoy_hbm, buoy)
     vel_load = load(vel_hbm, vin)
     lam_load = load(lam_hbm, lam)
@@ -122,14 +116,18 @@
             for first in (0, EDGE + depth):
                 ref[f, pl.ds(first * rows, EDGE * rows), :] = jnp.zeros((EDGE * rows, lanes), F32)
 
-    def clear_recv(*refs):
+    def clear_recv(way, *refs):
         for ref in refs:
-            ref[...] = jnp.zeros_like(ref)
-
-    pl.when(jnp.logical_not(has_prev_y))(functools.partial(clear_recv, up_recv))
-    pl.when(jnp.logical_not(has_next_y))(functools.partial(clear_recv, dn_recv))
-    pl.when(jnp.logical_not(has_prev_z))(functools.partial(clear_recv, zup_recv))
-    pl.when(jnp.logical_not(has_next_z))(functools.partial(clear_recv, zdn_recv))
+            for e in range(2 * STEPS):
+                ref[e, way] = jnp.zeros(ref.shape[2:], ref.dtype)
+
+    for exists, way, refs_of in (
+        (has_prev_y, 0, (ywhole_recv, ypart_recv)),
+        (has_next_y, 1, (ywhole_recv, ypart_recv)),
+        (has_prev_z, 0, (zwhole_recv, zpart_recv)),
+        (has_next_z, 1, (zwhole_recv, zpart_recv)),
+    ):
+        pl.when(jnp.logical_not(exists))(functools.partial(clear_recv, way, *refs_of))
 
     def set_damping():
         choice = prof_ref[0, 0, 0]
@@ -178,7 +176,7 @@
                 picker(k), cells.astype(BF16), (((1,), (1,)), ((), ())), preferred_element_type=F32
             )
             total = term if total is None else total + term
-        grp_send[e] = total
+        grp_send[e] = total.astype(BF16)
 
     def columns_copy(e):
         return pltpu.make_async_remote_copy(
@@ -187,7 +185,7 @@
         )
 
     def column_terms(e):
-        got = grp_recv[e].astype(BF16)
+        got = grp_recv[e]
         pair = jnp.concatenate([got, got], axis=0)
         return [
             lax.dot_general(pair, placer(k, forward), (((0,), (0,)), ((), ())), preferred_element_type=F32)
@@ -200,92 +198,81 @@
     def cell_row(ref, y):
         return ref.at[pl.ds(y, depth, stride=rows), :]
 
-    def rows_copy(e, upward, count):
-        src, dst = (up_send, up_recv) if upward else (dn_send, dn_recv)
-        way = 0 if upward else 1
-        return pltpu.make_async_remote_copy(
-            src_ref=src.at[e, pl.ds(0, count)], dst_ref=dst.at[e, pl.ds(0, count)],
-            send_sem=ysend_sem.at[e, way], recv_sem=yrecv_sem.at[e, way],
-            device_id=next_y if upward else prev_y, device_id_type=MESH,
-        )
-
-    def planes_copies(e, upward):
-        way, dst = (0, zup_recv) if upward else (1, zdn_recv)
-        copies = []
-        for k, (f, count, place) in enumerate(plane_list(kinds[e], upward)):
-            first = EDGE + depth - count if upward else EDGE
-            copies.append(pltpu.make_async_remote_copy(
-                src_ref=planes(refs[e], f, first, count),
-                dst_ref=dst.at[e, pl.ds(place * rows, count * rows), :],
-                send_sem=zsend_sem.at[e, way, k], recv_sem=zrecv_sem.at[e, way, k],
-                device_id=next_z if upward else prev_z, device_id_type=MESH,
-            ))
-        return copies
-
     kinds = (STRESS, MOTION) * STEPS
     refs = (s0, v1, s1, v2)
-
-    def start_rows(e):
-        kind = kinds[e]
-        pl.when(has_next_y)(lambda: rows_copy(e, True, len(row_list(kind, True))).start())
-        pl.when(has_prev_y)(lambda: rows_copy(e, False, len(row_list(kind, False))).start())
-
-    def start_planes(e):
-        for exists, upward in ((has_next_z, True), (has_prev_z, False)):
+    axes = {
+        "y": (
+            ywhole_send, ywhole_recv, ypart_send, ypart_recv, ysend_sem, yrecv_sem,
+            has_prev_y, has_next_y, prev_y, next_y,
+        ),
+        "z": (
+            zwhole_send, zwhole_recv, zpart_send, zpart_recv, zsend_sem, zrecv_sem,
+            has_prev_z, has_next_z, prev_z, next_z,
+        ),
+    }
+
+    def face_copies(e, axis, upward):
+        whole, whole_to, part, part_to, send_sem, recv_sem, _, _, before, after = axes[axis]
+        way = 0 if upward else 1
+        count = len(whole_list(kinds[e][axis], upward))
+        return [
+            pltpu.make_async_remote_copy(
+                src_ref=src, dst_ref=dst, send_sem=send_sem.at[e, way, i], recv_sem=recv_sem.at[e, way, i],
+                device_id=after if upward else before, device_id_type=MESH,
+            )
+            for i, (src, dst) in enumerate((
+                (whole.at[e, way, pl.ds(0, count)], whole_to.at[e, way, pl.ds(0, count)]),
+                (part.at[e, way], part_to.at[e, way]),
+            ))
+        ]
+
+    def each_copy(e, axis, outgoing, act):
+        has_before, has_after = axes[axis][6:8]
+        for exists, upward in ((has_after, outgoing), (has_before, not outgoing)):
             @pl.when(exists)
             def _():
-                for copy in planes_copies(e, upward):
-                    copy.start()
-
-    def wait_planes(e):
-        for exists, upward in ((has_prev_z, True), (has_next_z, False)):
-            @pl.when(exists)
-            def _():
-                for copy in planes_copies(e, upward):
-                    copy.wait_recv()
-
-    def wait_rows(e):
-        kind = kinds[e]
-        pl.when(has_prev_y)(lambda: rows_copy(e, True, len(row_list(kind, True))).wait_recv())
-        pl.when(has_next_y)(lambda: rows_copy(e, False, len(row_list(kind, False))).wait_recv())
-
-    def row_terms(e):
-        kind = kinds[e]
-        before = {(k, far): up_recv[e, place] for place, (k, _, far) in enumerate(row_list(kind, True))}
-        after = {(k, far): dn_recv[e, place] for place, (k, _, far) in enumerate(row_list(kind, False))}
-        return [
-            halo_terms(
-                forward,
-                [before[k, far] for far in range(2) if (k, far) in before],
-                [after[k, far] for far in range(2) if (k, far) in after],
-                rows,
-            )
-            for k, (_, forward) in enumerate(kind["y"])
-        ]
-
-    def plane_terms(e):
-        kind = kinds[e]
+                for copy in face_copies(e, axis, upward):
+                    act(copy)
+
+    def start_faces(e, axis):
+        each_copy(e, axis, True, lambda copy: copy.start())
+
+    def wait_faces(e, axis):
+        each_copy(e, axis, False, lambda copy: copy.wait_recv())
+
+    def fill_faces(e, axis, value):
+        whole, _, part, _ = axes[axis][:4]
+        fields = kinds[e][axis]
+        for way, upward in ((0, True), (1, False)):
+            last_index = (rows if axis == "y" else depth) - 1
+
+            def layer(k, far):
+                return value(fields[k][0], last_index - far if upward else far)
+
+            for place, k in enumerate(whole_list(fields, upward)):
+                whole[e, way, place] = layer(k, 0)
+            for k, (_, forward) in enumerate(fields):
+                part[e, way, k] = layer(k, part_depth(forward, upward)).astype(BF16)
+
+    def fill_rows(e, values):
+        fill_faces(e, "y", lambda f, y: row_at(refs[e], f, y)[...] if (f, y) not in values else values[f, y])
+
+    def fill_planes(e):
+        fill_faces(e, "z", lambda f, z: refs[e][f, pl.ds((z + EDGE) * rows, rows), :])
+
+    def face_terms(e, axis):
+        _, whole, _, part = axes[axis][:4]
+        fields = kinds[e][axis]
         terms = []
-        for k, (_, forward) in enumerate(kind["z"]):
+        for k, (_, forward) in enumerate(fields):
             layers = []
-            for upward, ref in ((True, zup_recv), (False, zdn_recv)):
-                _, count, place = plane_list(kind, upward)[k]
-                got = [ref[e, pl.ds((place + i) * rows, rows), :] for i in range(count)]
-                layers.append(got[::-1] if upward else got)
-            terms.append(halo_terms(forward, *layers, depth))
+            for way, upward in ((0, True), (1, False)):
+                got = [part[e, way, k].astype(F32)]
+                if forward != upward:
+                    got.insert(0, whole[e, way, whole_list(fields, upward).index(k)])
+                layers.append(got)
+            terms.append(halo_terms(forward, *layers, rows if axis == "y" else depth))
         return terms
-
-    def fill_rows(e, values):
-        kind, ref = kinds[e], refs[e]
-
-        def value(field, y):
-            got = values.get((field, y))
-            return row_at(ref, field, y)[...] if got is None else got
-
-        for place, (_, field, far) in enumerate(row_list(kind, True)):
-            up_send[e, place] = value(field, rows - 1 - far)
-        for place, (_, field, far) in enumerate(row_list(kind, False)):
-            dn_send[e, place] = value(field, far)
 
     lane_id = lax.broadcasted_iota(jnp.int32, (rows, lanes), 1)
     row_id = lax.broadcasted_iota(jnp.int32, (rows, lanes), 0)
@@ -374,16 +361,17 @@
     for f in (1, 3, 4):
         stress_load[f].wait()
     fill_rows(0, {})
-    for f in (0, 2):
+    for f in (2, 5):
         stress_load[f].wait()
-    send_columns(0, STRESS, s0)
-    stress_load[5].wait()
+    fill_planes(0)
+    stress_load[0].wait()
 
     neighbours = 1 + sum(e.astype(jnp.int32) for e in (has_prev_y, has_next_y, has_prev_z, has_next_z))
     pl.semaphore_wait(barrier, neighbours)
-    start_rows(0)
+    start_faces(0, "y")
+    start_faces(0, "z")
+    send_columns(0, STRESS, s0)
     columns_copy(0).start()
-    start_planes(0)
 
     for copy in (peak_load, buoy_load, vel_load, lam_load, mu_load):
         copy.wait()
@@ -406,25 +394,26 @@
         e = 2 * step
         src, old, new = (s0, vin, v1) if step == 0 else (s1, v1, v2)
         planes_loop(functools.partial(motion_plane, src, old_motion(old), new))
-        wait_planes(e)
-        for k, terms in enumerate(plane_terms(e)):
-            for z, term in terms.items():
-                cells = new.at[k, pl.ds((z + EDGE) * rows, rows), :]
-                cells[...] = cells[...] + buoy[pl.ds(z * rows, rows), :] * term
         columns_copy(e).wait_recv()
         for k, term in enumerate(column_terms(e)):
             cells = interior(new, k)
             cells[...] = cells[...] + buoy[...] * term
-        wait_rows(e)
+        wait_faces(e, "z")
+        for k, terms in enumerate(face_terms(e, "z")):
+            for z, term in terms.items():
+                cells = new.at[k, pl.ds((z + EDGE) * rows, rows), :]
+                cells[...] = cells[...] + buoy[pl.ds(z * rows, rows), :] * term
+        wait_faces(e, "y")
         values = {}
-        for k, terms in enumerate(row_terms(e)):
+        for k, terms in enumerate(face_terms(e, "y")):
             for y, term in terms.items():
                 got = row_at(new, k, y)[...] + cell_row(buoy, y)[...] * term
                 row_at(new, k, y)[...] = got
                 values[k, y] = got
         fill_rows(e + 1, values)
-        start_rows(e + 1)
-        start_planes(e + 1)
+        start_faces(e + 1, "y")
+        fill_planes(e + 1)
+        start_faces(e + 1, "z")
         send_columns(e + 1, MOTION, new)
         columns_copy(e + 1).start()
 
@@ -465,8 +454,16 @@
             planes_loop(body)
 
         planes_loop(functools.partial(tensor_plane, src, old_tensor, store))
-        wait_planes(e)
-        for k, terms in enumerate(plane_terms(e)):
+        columns_copy(e).wait_recv()
+        for k, term in enumerate(column_terms(e)):
+            correct(
+                STRAIN["x"][k], term,
+                lambda f: sfin.at[f] if last else interior(s1, f),
+                lambda ref: ref,
+                lambda f: strain.at[f],
+            )
+        wait_faces(e, "z")
+        for k, terms in enumerate(face_terms(e, "z")):
             for z, term in terms.items():
                 cell = pl.ds(z * rows, rows)
                 correct(
@@ -475,48 +472,50 @@
                     lambda ref: ref.at[cell, :],
                     lambda f: strain.at[f, cell, :],
                 )
-        columns_copy(e).wait_recv()
-        for k, term in enumerate(column_terms(e)):
-            correct(
-                STRAIN["x"][k], term,
-                lambda f: sfin.at[f] if last else interior(s1, f),
-                lambda ref: ref,
-                lambda f: strain.at[f],
-            )
         if last:
             convert((0, 2, 5))
-        wait_rows(e)
-        values = {}
-        for k, terms in enumerate(row_terms(e)):
+        wait_faces(e, "y")
+
+        def stress_row(f, y):
+            return cell_row(sfin.at[f], y) if last else row_at(s1, f, y)
+
+        def change(f, y, amount):
+            got = stress_row(f, y)[...] + amount
+            stress_row(f, y)[...] = got
+            return got
+
+        shear_xy, normal_y, shear_yz = face_terms(e, "y")
+        values, spread = {}, {}
+        for f, terms in ((1, shear_xy), (4, shear_yz)):
             for y, term in terms.items():
-                changed = correct(
-                    STRAIN["y"][k], term,
-                    lambda f: cell_row(sfin.at[f], y) if last else row_at(s1, f, y),
-                    lambda ref: cell_row(ref, y),
-                    lambda f: cell_row(strain.at[f], y),
-                )
-                for f, got in changed.items():
-                    values[f, y] = got
-        if last:
-            convert((1, 3, 4))
-        else:
+                values[f, y] = change(f, y, cell_row(mu, y)[...] * term)
+        for y, term in normal_y.items():
+            mu_row = cell_row(mu, y)[...]
+            spread[y] = cell_row(lam, y)[...] * term
+            values[3, y] = change(3, y, spread[y] + (mu_row + mu_row) * term)
+        if not last:
             fill_rows(e + 1, values)
-            start_rows(e + 1)
-            start_planes(e + 1)
+            start_faces(e + 1, "y")
+        for y, amount in spread.items():
+            change(5, y, amount)
+        if not last:
+            fill_planes(e + 1)
+            start_faces(e + 1, "z")
+        for y, amount in spread.items():
+            change(0, y, amount)
+        if not last:
             send_columns(e + 1, STRESS, s1)
             columns_copy(e + 1).start()
-            convert(range(6))
+        for f, terms in ((1, shear_xy), (3, normal_y), (4, shear_yz)):
+            for y, term in terms.items():
+                place = cell_row(strain.at[f], y)
+                place[...] = place[...] + term
+        convert((1, 3, 4) if last else range(6))
 
     for e in range(2 * STEPS):
-        kind = kinds[e]
         columns_copy(e).wait_send()
-        pl.when(has_next_y)(lambda: rows_copy(e, True, len(row_list(kind, True))).wait_send())
-        pl.when(has_prev_y)(lambda: rows_copy(e, False, len(row_list(kind, False))).wait_send())
-        for exists, upward in ((has_next_z, True), (has_prev_z, False)):
-            @pl.when(exists)
-            def _():
-                for copy in planes_copies(e, upward):
-                    copy.wait_send()
+        for axis in axes:
+            each_copy(e, axis, True, lambda copy: copy.wait_send())
 
 
 def write_out(v2, sfin, eout, vout_hbm, sout_hbm, eout_hbm, sem):
@@ -571,21 +570,14 @@
             pltpu.VMEM((depth, 8, lanes), F32),
             pltpu.VMEM((6, cells, lanes), F32),
             pltpu.SMEM(damping_peak.shape, F32),
-            pltpu.VMEM((exchanges, 5, depth, lanes), F32),
-            pltpu.VMEM((exchanges, 5, depth, lanes), F32),
-            pltpu.VMEM((exchanges, 5, depth, lanes), F32),
-            pltpu.VMEM((exchanges, 5, depth, lanes), F32),
-            pltpu.VMEM((exchanges, 5 * rows, lanes), F32),
-            pltpu.VMEM((exchanges, 5 * rows, lanes), F32),
-            pltpu.VMEM((exchanges, 8, cells), F32),
-            pltpu.VMEM((exchanges, 8, cells), F32),
+            *[pltpu.VMEM((exchanges, 2, 2, depth, lanes), F32)] * 2,
+            *[pltpu.VMEM((exchanges, 2, 3, depth, lanes), BF16)] * 2,
+            *[pltpu.VMEM((exchanges, 2, 2, rows, lanes), F32)] * 2,
+            *[pltpu.VMEM((exchanges, 2, 3, rows, lanes), BF16)] * 2,
+            *[pltpu.VMEM((exchanges, 8, cells), BF16)] * 2,
             dma((11,)),
-            dma((exchanges, 2)),
-            dma((exchanges, 2)),
-            dma((exchanges, 2, 3)),
-            dma((exchanges, 2, 3)),
-            dma((exchanges,)),
-            dma((exchanges,)),
+            *[dma((exchanges, 2, 2))] * 4,
+            *[dma((exchanges,))] * 2,
         ],
         compiler_params=pltpu.CompilerParams(
             collective_id=0, has_side_effects=True, vmem_limit_bytes=VMEM_LIMIT

time: 30 us -> 28.8 us (0.960)
  Pallas kernels: 27.9 us -> 26.7 us
    pallas_call x1, Pallas kernels: 26.5 us -> 25.3 us  [on_device(): pl.pallas_call(functools.partial(kernel, depth, rows, lanes), out_shape=(...]
where the time goes in v3:
time: 28.8 us; the launch traced here: 28.6 us
  Pallas kernels  26.7 us (93%)
  between operations  1.93 us (7%)
    pallas_call x1, Pallas kernels, on_device(): pl.pallas_call(functools.partial(kernel, depth, rows, lanes), out_shape=(...  25.3 us
    pallas_call x1, Pallas kernels, on_device(): pl.pallas_call(write_out, out_shape=(jax.ShapeDtypeStruct((3, cells, lane...  1.44 us

profile of v3, /device:TPU:199, one launch (start us, length us, event | category | flops | bytes accessed | tf_op | source)
XLA Modules:
  0.0 28.6 jit_solution(2407542519770202677)
XLA Ops:
  1.9 25.3 %two_steps.1 = (f32[3,320,128]{2,1,0:T(8,128)S(1)}, f32[6,256,128]{2,1,0:T(8,128)S(1)}, bf16[12,256,128]{2,1,0:T(8,128)(2,1)S(1)}) custom-call(f32[3,256,128]{2,1,0:T(8,128)} %bitcast.9, f32[6,256,128]{2,1,0:T(8,128)} %bitcast.8, f32[256,128]{1,0:T(8,128)} %bitcast.10, f32[256,128]{1,0:T(8,128)} %bitcast.11, f32[256,128]{1,0:T(8,128)} %bitcast.12, ...), custom_call_target="tpu_custom_call" | custom-call | tf_op jit(solution)/shard_map/two_steps/pallas_call | solution.py:552
  27.2 1.4 %write_out.1 = (f32[3,256,128]{2,1,0:T(8,128)}, f32[6,256,128]{2,1,0:T(8,128)}, bf16[12,256,128]{2,1,0:T(8,128)(2,1)}) custom-call(f32[3,320,128]{2,1,0:T(8,128)S(1)} %get-tuple-element.9.v2, f32[6,256,128]{2,1,0:T(8,128)S(1)} %get-tuple-element.10.sfin, bf16[12,256,128]{2,1,0:T(8,128)(2,1)S(1)} %get-tuple-element.11.eout), custom_call_target="tpu_custom_call" | custom-call | tf_op jit(solution)/shard_map/write_out/pallas_call | solution.py:601

commit v4 on v3

--- a/solution.py
+++ b/solution.py
@@ -65,8 +65,8 @@
     v2, sfin, eout,
     s0, s1, v1, vin, buoy, lam, mu, keep_ref, gain_ref, strain, peak_ref,
     ywhole_send, ywhole_recv, ypart_send, ypart_recv, zwhole_send, zwhole_recv, zpart_send, zpart_recv,
-    grp_send, grp_recv,
-    in_sem, ysend_sem, yrecv_sem, zsend_sem, zrecv_sem, gsend_sem, grecv_sem,
+    coef_send, coef_recv, grp_send, grp_recv,
+    in_sem, ysend_sem, yrecv_sem, zsend_sem, zrecv_sem, csend_sem, crecv_sem, gsend_sem, grecv_sem,
 ):
     gx, gy, grp = lax.axis_index("gx"), lax.axis_index("gy"), lax.axis_index("grp")
     n_gx, n_gy = lax.axis_size("gx"), lax.axis_size("gy")
@@ -128,6 +128,12 @@
         (has_next_z, 1, (zwhole_recv, zpart_recv)),
     ):
         pl.when(jnp.logical_not(exists))(functools.partial(clear_recv, way, *refs_of))
+
+    def clear_coef(way):
+        coef_recv[way] = jnp.zeros(coef_recv.shape[1:], F32)
+
+    pl.when(jnp.logical_not(has_prev_y))(functools.partial(clear_coef, 0))
+    pl.when(jnp.logical_not(has_next_y))(functools.partial(clear_coef, 1))
 
     def set_damping():
         choice = prof_ref[0, 0, 0]
@@ -254,13 +260,61 @@
             for k, (_, forward) in enumerate(fields):
                 part[e, way, k] = layer(k, part_depth(forward, upward)).astype(BF16)
 
-    def fill_rows(e, values):
-        fill_faces(e, "y", lambda f, y: row_at(refs[e], f, y)[...] if (f, y) not in values else values[f, y])
+    def fill_rows(e):
+        fill_faces(e, "y", lambda f, y: row_at(refs[e], f, y)[...])
 
     def fill_planes(e):
         fill_faces(e, "z", lambda f, z: refs[e][f, pl.ds((z + EDGE) * rows, rows), :])
 
-    def face_terms(e, axis):
+    def material_row(k, stress, y):
+        if not stress:
+            return cell_row(buoy, y)[...]
+        if k == 1:
+            mu_row = cell_row(mu, y)[...]
+            return cell_row(lam, y)[...] + (mu_row + mu_row)
+        return cell_row(mu, y)[...]
+
+    def fill_material():
+        for way, (near, far) in ((0, (rows - 1, rows - 2)), (1, (0, 1))):
+            coef_send[way, 0] = material_row(0, False, near)
+            coef_send[way, 1] = material_row(0, False, far)
+            coef_send[way, 2] = material_row(0, True, near)
+            coef_send[way, 3] = material_row(1, True, near)
+            coef_send[way, 4] = material_row(way, True, far)
+
+    def material_copy(way):
+        return pltpu.make_async_remote_copy(
+            src_ref=coef_send.at[way], dst_ref=coef_recv.at[way],
+            send_sem=csend_sem.at[way], recv_sem=crecv_sem.at[way],
+            device_id=prev_y if way else next_y, device_id_type=MESH,
+        )
+
+    def completions(e):
+        if e == 0:
+            return {}
+        missing = {}
+        for way, upward in ((0, True), (1, False)):
+            near, far = (0, 1) if upward else (rows - 1, rows - 2)
+            sign = 1.0 if upward else -1.0
+
+            def coef(k, layer):
+                if kinds[e] is MOTION:
+                    return coef_recv[way, layer]
+                return coef_recv[way, 4 if layer else (3 if k == 1 else 2)]
+
+            for k, (_, forward) in enumerate(kinds[e]["y"]):
+                driver = kinds[e - 1]["y"][k][0]
+                near_row = row_at(refs[e - 1], driver, near)[...]
+                part = (sign * RATIO) * near_row
+                if forward != upward:
+                    far_row = row_at(refs[e - 1], driver, far)[...]
+                    missing[way, k, 0] = coef(k, 0) * (sign * near_row + (sign * RATIO) * far_row)
+                    missing[way, k, 1] = coef(k, 1) * part
+                else:
+                    missing[way, k, 0] = coef(k, 0) * part
+        return missing
+
+    def face_terms(e, axis, missing=None):
         _, whole, _, part = axes[axis][:4]
         fields = kinds[e][axis]
         terms = []
@@ -270,6 +324,8 @@
                 got = [part[e, way, k].astype(F32)]
                 if forward != upward:
                     got.insert(0, whole[e, way, whole_list(fields, upward).index(k)])
+                if missing:
+                    got = [layer + missing[way, k, i] for i, layer in enumerate(got)]
                 layers.append(got)
             terms.append(halo_terms(forward, *layers, rows if axis == "y" else depth))
         return terms
@@ -360,7 +416,7 @@
 
     for f in (1, 3, 4):
         stress_load[f].wait()
-    fill_rows(0, {})
+    fill_rows(0)
     for f in (2, 5):
         stress_load[f].wait()
     fill_planes(0)
@@ -383,6 +439,9 @@
             ref[plane(z), :] = gain * ref[plane(z), :]
 
     planes_loop(scale)
+    fill_material()
+    pl.when(has_next_y)(lambda: material_copy(0).start())
+    pl.when(has_prev_y)(lambda: material_copy(1).start())
 
     def old_motion(ref):
         if ref is vin:
@@ -403,15 +462,13 @@
             for z, term in terms.items():
                 cells = new.at[k, pl.ds((z + EDGE) * rows, rows), :]
                 cells[...] = cells[...] + buoy[pl.ds(z * rows, rows), :] * term
+        fill_rows(e + 1)
+        start_faces(e + 1, "y")
+        missing = completions(e)
         wait_faces(e, "y")
-        values = {}
-        for k, terms in enumerate(face_terms(e, "y")):
+        for k, terms in enumerate(face_terms(e, "y", missing)):
             for y, term in terms.items():
-                got = row_at(new, k, y)[...] + cell_row(buoy, y)[...] * term
-                row_at(new, k, y)[...] = got
-                values[k, y] = got
-        fill_rows(e + 1, values)
-        start_faces(e + 1, "y")
+                row_at(new, k, y)[...] = row_at(new, k, y)[...] + cell_row(buoy, y)[...] * term
         fill_planes(e + 1)
         start_faces(e + 1, "z")
         send_columns(e + 1, MOTION, new)
@@ -474,6 +531,13 @@
                 )
         if last:
             convert((0, 2, 5))
+        else:
+            fill_rows(e + 1)
+            start_faces(e + 1, "y")
+        if e == 1:
+            pl.when(has_prev_y)(lambda: material_copy(0).wait_recv())
+            pl.when(has_next_y)(lambda: material_copy(1).wait_recv())
+        missing = completions(e)
         wait_faces(e, "y")
 
         def stress_row(f, y):
@@ -484,18 +548,10 @@
             stress_row(f, y)[...] = got
             return got
 
-        shear_xy, normal_y, shear_yz = face_terms(e, "y")
-        values, spread = {}, {}
-        for f, terms in ((1, shear_xy), (4, shear_yz)):
-            for y, term in terms.items():
-                values[f, y] = change(f, y, cell_row(mu, y)[...] * term)
-        for y, term in normal_y.items():
-            mu_row = cell_row(mu, y)[...]
-            spread[y] = cell_row(lam, y)[...] * term
-            values[3, y] = change(3, y, spread[y] + (mu_row + mu_row) * term)
-        if not last:
-            fill_rows(e + 1, values)
-            start_faces(e + 1, "y")
+        shear_xy, normal_y, shear_yz = face_terms(e, "y", missing)
+        spread = {y: cell_row(lam, y)[...] * term for y, term in normal_y.items()}
+        for y, term in shear_yz.items():
+            change(4, y, cell_row(mu, y)[...] * term)
         for y, amount in spread.items():
             change(5, y, amount)
         if not last:
@@ -503,9 +559,14 @@
             start_faces(e + 1, "z")
         for y, amount in spread.items():
             change(0, y, amount)
+        for y, term in shear_xy.items():
+            change(1, y, cell_row(mu, y)[...] * term)
         if not last:
             send_columns(e + 1, STRESS, s1)
             columns_copy(e + 1).start()
+        for y, term in normal_y.items():
+            mu_row = cell_row(mu, y)[...]
+            change(3, y, spread[y] + (mu_row + mu_row) * term)
         for f, terms in ((1, shear_xy), (3, normal_y), (4, shear_yz)):
             for y, term in terms.items():
                 place = cell_row(strain.at[f], y)
@@ -516,6 +577,8 @@
         columns_copy(e).wait_send()
         for axis in axes:
             each_copy(e, axis, True, lambda copy: copy.wait_send())
+    pl.when(has_next_y)(lambda: material_copy(0).wait_send())
+    pl.when(has_prev_y)(lambda: material_copy(1).wait_send())
 
 
 def write_out(v2, sfin, eout, vout_hbm, sout_hbm, eout_hbm, sem):
@@ -574,9 +637,11 @@
             *[pltpu.VMEM((exchanges, 2, 3, depth, lanes), BF16)] * 2,
             *[pltpu.VMEM((exchanges, 2, 2, rows, lanes), F32)] * 2,
             *[pltpu.VMEM((exchanges, 2, 3, rows, lanes), BF16)] * 2,
+            *[pltpu.VMEM((2, 5, depth, lanes), F32)] * 2,
             *[pltpu.VMEM((exchanges, 8, cells), BF16)] * 2,
             dma((11,)),
             *[dma((exchanges, 2, 2))] * 4,
+            *[dma((2,))] * 2,
             *[dma((exchanges,))] * 2,
         ],
         compiler_params=pltpu.CompilerParams(

time: 28.8 us -> 27.7 us (0.962)
  Pallas kernels: 26.7 us -> 25.6 us
    pallas_call x1, Pallas kernels: 25.3 us -> 24.1 us  [on_device(): pl.pallas_call(functools.partial(kernel, depth, rows, lanes), out_shape=(...]
where the time goes in v4:
time: 27.7 us; the launch traced here: 27.5 us
  Pallas kernels  25.6 us (92%)
  between operations  1.93 us (7%)
    pallas_call x1, Pallas kernels, on_device(): pl.pallas_call(functools.partial(kernel, depth, rows, lanes), out_shape=(...  24.1 us
    pallas_call x1, Pallas kernels, on_device(): pl.pallas_call(write_out, out_shape=(jax.ShapeDtypeStruct((3, cells, lane...  1.44 us

profile of v4, /device:TPU:199, one launch (start us, length us, event | category | flops | bytes accessed | tf_op | source)
XLA Modules:
  0.0 27.5 jit_solution(8382170189513705389)
XLA Ops:
  1.9 24.1 %two_steps.1 = (f32[3,320,128]{2,1,0:T(8,128)S(1)}, f32[6,256,128]{2,1,0:T(8,128)S(1)}, bf16[12,256,128]{2,1,0:T(8,128)(2,1)S(1)}) custom-call(f32[3,256,128]{2,1,0:T(8,128)} %bitcast.9, f32[6,256,128]{2,1,0:T(8,128)} %bitcast.8, f32[256,128]{1,0:T(8,128)} %bitcast.10, f32[256,128]{1,0:T(8,128)} %bitcast.11, f32[256,128]{1,0:T(8,128)} %bitcast.12, ...), custom_call_target="tpu_custom_call" | custom-call | tf_op jit(solution)/shard_map/two_steps/pallas_call | solution.py:615
  26.1 1.4 %write_out.1 = (f32[3,256,128]{2,1,0:T(8,128)}, f32[6,256,128]{2,1,0:T(8,128)}, bf16[12,256,128]{2,1,0:T(8,128)(2,1)}) custom-call(f32[3,320,128]{2,1,0:T(8,128)S(1)} %get-tuple-element.9.v2, f32[6,256,128]{2,1,0:T(8,128)S(1)} %get-tuple-element.10.sfin, bf16[12,256,128]{2,1,0:T(8,128)(2,1)S(1)} %get-tuple-element.11.eout), custom_call_target="tpu_custom_call" | custom-call | tf_op jit(solution)/shard_map/write_out/pallas_call | solution.py:666

commit v5 on v4

--- a/solution.py
+++ b/solution.py
@@ -169,10 +169,13 @@
             after = (near & (lane == lanes - 1)) & (grp == 0)
             before = ((near & (lane == 1)) | (far & (lane == 0))) & (grp == 1)
             whole = jnp.where(one, -1.0, 0.0)
-        part = jnp.where(after, RATIO, jnp.where(before, -RATIO, 0.0))
-        high = part.astype(BF16)
-        low = (part - high.astype(F32)).astype(BF16)
-        return jnp.concatenate([whole.astype(BF16) + high, low], axis=0)
+        return whole + jnp.where(after, RATIO, jnp.where(before, -RATIO, 0.0))
+
+    def placer_of(kind):
+        total = sum(pltpu.roll(placer(k, forward), lanes - 2 * k, 1) if k else placer(k, forward)
+                    for k, (_, forward) in enumerate(kind["x"]))
+        high = total.astype(BF16)
+        return jnp.concatenate([high, (total - high.astype(F32)).astype(BF16)], axis=0)
 
     def send_columns(e, kind, ref):
         total = None
@@ -193,10 +196,13 @@
     def column_terms(e):
         got = grp_recv[e]
         pair = jnp.concatenate([got, got], axis=0)
-        return [
-            lax.dot_general(pair, placer(k, forward), (((0,), (0,)), ((), ())), preferred_element_type=F32)
-            for k, (_, forward) in enumerate(kinds[e]["x"])
-        ]
+        total = lax.dot_general(
+            pair, placer_of(kinds[e]), (((0,), (0,)), ((), ())), preferred_element_type=F32
+        )
+        at = lax.broadcasted_iota(jnp.int32, total.shape, 1)
+        edge = (at >= lanes - 2) == (grp == 0)
+        edge = edge & ((at >= lanes - 2) | (at < 2))
+        return [jnp.where(edge, pltpu.roll(total, 2 * k, 1) if k else total, 0.0) for k in range(3)]
 
     def row_at(ref, field, y):
         return ref.at[field, pl.ds(EDGE * rows + y, depth, stride=rows), :]
@@ -440,8 +446,6 @@
 
     planes_loop(scale)
     fill_material()
-    pl.when(has_next_y)(lambda: material_copy(0).start())
-    pl.when(has_prev_y)(lambda: material_copy(1).start())
 
     def old_motion(ref):
         if ref is vin:
@@ -453,6 +457,9 @@
         e = 2 * step
         src, old, new = (s0, vin, v1) if step == 0 else (s1, v1, v2)
         planes_loop(functools.partial(motion_plane, src, old_motion(old), new))
+        if step == 0:
+            pl.when(has_next_y)(lambda: material_copy(0).start())
+            pl.when(has_prev_y)(lambda: material_copy(1).start())
         columns_copy(e).wait_recv()
         for k, term in enumerate(column_terms(e)):
             cells = interior(new, k)

time: 27.7 us -> 27.6 us (level)
  no operation moved by 1% of the time
where the time goes in v5:
time: 27.6 us; the launch traced here: 27.4 us
  Pallas kernels  25.5 us (92%)
  between operations  1.93 us (7%)
    pallas_call x1, Pallas kernels, on_device(): pl.pallas_call(functools.partial(kernel, depth, rows, lanes), out_shape=(...  24.1 us
    pallas_call x1, Pallas kernels, on_device(): pl.pallas_call(write_out, out_shape=(jax.ShapeDtypeStruct((3, cells, lane...  1.44 us

profile of v5, /device:TPU:199, one launch (start us, length us, event | category | flops | bytes accessed | tf_op | source)
XLA Modules:
  0.0 27.4 jit_solution(1095580193928065075)
XLA Ops:
  1.9 24.1 %two_steps.1 = (f32[3,320,128]{2,1,0:T(8,128)S(1)}, f32[6,256,128]{2,1,0:T(8,128)S(1)}, bf16[12,256,128]{2,1,0:T(8,128)(2,1)S(1)}) custom-call(f32[3,256,128]{2,1,0:T(8,128)} %bitcast.9, f32[6,256,128]{2,1,0:T(8,128)} %bitcast.8, f32[256,128]{1,0:T(8,128)} %bitcast.10, f32[256,128]{1,0:T(8,128)} %bitcast.11, f32[256,128]{1,0:T(8,128)} %bitcast.12, ...), custom_call_target="tpu_custom_call" | custom-call | tf_op jit(solution)/shard_map/two_steps/pallas_call | solution.py:622
  26.0 1.4 %write_out.1 = (f32[3,256,128]{2,1,0:T(8,128)}, f32[6,256,128]{2,1,0:T(8,128)}, bf16[12,256,128]{2,1,0:T(8,128)(2,1)}) custom-call(f32[3,320,128]{2,1,0:T(8,128)S(1)} %get-tuple-element.9.v2, f32[6,256,128]{2,1,0:T(8,128)S(1)} %get-tuple-element.10.sfin, bf16[12,256,128]{2,1,0:T(8,128)(2,1)S(1)} %get-tuple-element.11.eout), custom_call_target="tpu_custom_call" | custom-call | tf_op jit(solution)/shard_map/write_out/pallas_call | solution.py:673

commit v6 on v5

--- a/solution.py
+++ b/solution.py
@@ -418,7 +418,7 @@
             body(z)
             return carry
 
-        lax.fori_loop(0, depth, step, 0, unroll=2)
+        lax.fori_loop(0, depth, step, 0)
 
     for f in (1, 3, 4):
         stress_load[f].wait()
@@ -538,6 +538,12 @@
                 )
         if last:
             convert((0, 2, 5))
+            for sent in range(2 * STEPS):
+                columns_copy(sent).wait_send()
+                for axis in axes:
+                    each_copy(sent, axis, True, lambda copy: copy.wait_send())
+            pl.when(has_next_y)(lambda: material_copy(0).wait_send())
+            pl.when(has_prev_y)(lambda: material_copy(1).wait_send())
         else:
             fill_rows(e + 1)
             start_faces(e + 1, "y")
@@ -579,13 +585,6 @@
                 place = cell_row(strain.at[f], y)
                 place[...] = place[...] + term
         convert((1, 3, 4) if last else range(6))
-
-    for e in range(2 * STEPS):
-        columns_copy(e).wait_send()
-        for axis in axes:
-            each_copy(e, axis, True, lambda copy: copy.wait_send())
-    pl.when(has_next_y)(lambda: material_copy(0).wait_send())
-    pl.when(has_prev_y)(lambda: material_copy(1).wait_send())
 
 
 def write_out(v2, sfin, eout, vout_hbm, sout_hbm, eout_hbm, sem):

time: 27.6 us -> 27.7 us (level)
  no operation moved by 1% of the time
where the time goes in v6:
time: 27.7 us; the launch traced here: 27.5 us
  Pallas kernels  25.6 us (92%)
  between operations  1.93 us (7%)
    pallas_call x1, Pallas kernels, on_device(): pl.pallas_call(functools.partial(kernel, depth, rows, lanes), out_shape=(...  24.1 us
    pallas_call x1, Pallas kernels, on_device(): pl.pallas_call(write_out, out_shape=(jax.ShapeDtypeStruct((3, cells, lane...  1.44 us

profile of v6, /device:TPU:199, one launch (start us, length us, event | category | flops | bytes accessed | tf_op | source)
XLA Modules:
  0.0 27.5 jit_solution(8225895091985901262)
XLA Ops:
  1.9 24.1 %two_steps.1 = (f32[3,320,128]{2,1,0:T(8,128)S(1)}, f32[6,256,128]{2,1,0:T(8,128)S(1)}, bf16[12,256,128]{2,1,0:T(8,128)(2,1)S(1)}) custom-call(f32[3,256,128]{2,1,0:T(8,128)} %bitcast.9, f32[6,256,128]{2,1,0:T(8,128)} %bitcast.8, f32[256,128]{1,0:T(8,128)} %bitcast.10, f32[256,128]{1,0:T(8,128)} %bitcast.11, f32[256,128]{1,0:T(8,128)} %bitcast.12, ...), custom_call_target="tpu_custom_call" | custom-call | tf_op jit(solution)/shard_map/two_steps/pallas_call | solution.py:621
  26.1 1.4 %write_out.1 = (f32[3,256,128]{2,1,0:T(8,128)}, f32[6,256,128]{2,1,0:T(8,128)}, bf16[12,256,128]{2,1,0:T(8,128)(2,1)}) custom-call(f32[3,320,128]{2,1,0:T(8,128)S(1)} %get-tuple-element.9.v2, f32[6,256,128]{2,1,0:T(8,128)S(1)} %get-tuple-element.10.sfin, bf16[12,256,128]{2,1,0:T(8,128)(2,1)S(1)} %get-tuple-element.11.eout), custom_call_target="tpu_custom_call" | custom-call | tf_op jit(solution)/shard_map/write_out/pallas_call | solution.py:672
